TPU v7x, 32 devices: a whole 2x2x4 slice. The times are simulated.
32 devices in a mesh: mod: 2 (over x), page: 16 (over z, y, core).
Axes of the slice: x: 2, y: 2, z: 4, core: 2. Of those that a mesh axis runs over, the one named last changes fastest.
Arguments:
- states: bfloat16 [2, 16, 512, 768], P('mod', 'page'), may hold values from -6 to 6
- cotangent: bfloat16 [2, 16, 512, 768], P('mod', 'page'), may hold values from -6 to 6
- segments: int32 [16, 512], P('page'), may hold values from 0 to 7, never falling along the last dimension, each value on 1 to 128 neighbouring positions
- box_x: int32 [16, 512], P('page'), may hold values from 0 to 31
- box_y: int32 [16, 512], P('page'), may hold values from 0 to 31
- conv_weight: float32 [3, 768], replicated, may hold values from -3 to 3
- conv_bias: float32 [768], replicated, may hold values from -2 to 2
- w_query: bfloat16 [768, 768], P('page'), may hold values from -0.21875 to 0.21875
- b_query: float32 [768], replicated, may hold values from -3 to 3
- w_key: bfloat16 [768, 768], P('page'), may hold values from -0.21875 to 0.21875
- w_value: bfloat16 [768, 768], P('page'), may hold values from -0.21875 to 0.21875
- b_value: float32 [768], replicated, may hold values from -3 to 3
- w_out: bfloat16 [768, 768], P('page'), may hold values from -0.875 to 0.875
- b_out: float32 [768], replicated, may hold values from -2 to 2
- table_pos: float32 [12, 127], replicated, may hold values from -3 to 3
- table_x: float32 [12, 63], replicated, may hold values from -3 to 3
- table_y: float32 [12, 63], replicated, may hold values from -3 to 3
- gain_one: float32 [768], replicated, may hold values from 0.5 to 1.5
- bias_one: float32 [768], replicated, may hold values from -2 to 2
- w_up: bfloat16 [768, 3072], P('page'), may hold values from -0.21875 to 0.21875
- b_up: float32 [3072], replicated, may hold values from -3 to 3
- w_down: bfloat16 [3072, 768], P('page'), may hold values from -0.109375 to 0.109375
- b_down: float32 [768], replicated, may hold values from -2 to 2
- gain_two: float32 [768], replicated, may hold values from 0.5 to 1.5
- bias_two: float32 [768], replicated, may hold values from -2 to 2
Outputs:
- output: bfloat16 [2, 16, 512, 768], P('mod', 'page')
- grad_states: bfloat16 [2, 16, 512, 768], P('mod', 'page')
- grad_conv_weight: float32 [3, 768], replicated
- grad_conv_bias: float32 [768], replicated
- grad_w_query: float32 [768, 768], P('page')
- grad_b_query: float32 [768], replicated
- grad_w_key: float32 [768, 768], P('page')
- grad_w_value: float32 [768, 768], P('page')
- grad_b_value: float32 [768], replicated
- grad_w_out: float32 [768, 768], P('page')
- grad_b_out: float32 [768], replicated
- grad_table_pos: float32 [12, 127], replicated
- grad_table_x: float32 [12, 63], replicated
- grad_table_y: float32 [12, 63], replicated
- grad_gain_one: float32 [768], replicated
- grad_bias_one: float32 [768], replicated
- grad_w_up: float32 [768, 3072], P('page')
- grad_b_up: float32 [3072], replicated
- grad_w_down: float32 [3072, 768], P('page')
- grad_b_down: float32 [768], replicated
- grad_gain_two: float32 [768], replicated
- grad_bias_two: float32 [768], replicated
Inputs may be any that keep to these rules, and one draw needn't show every extreme that they name: `segments`: in each row the page ids never fall and each of the 8 pages has 1 to 128 text tokens, one page exactly 128.
All inputs are finite; a program needn't handle non-finite values.
Results may differ from a plain program's by a relative error of at most 0.017.
The roundings to bfloat16 on the way count: a program that leaves them out, or rounds other values in their place, can miss the bound.
Values may be sent and summed in bfloat16 or wider, within the bound.
No kernel may reach another device: no remote copies, remote signals or barrier semaphores. Data moves between devices by JAX's collectives and lax.ppermute only.
A program may use at most 192 MiB of HBM per device.

v0:
```python
import functools

import jax
import jax.numpy as jnp
import numpy as np
from jax import lax
from jax.experimental import pallas as pl
from jax.experimental.pallas import tpu as pltpu
from jax.sharding import PartitionSpec as P

HEADS = 12
HEAD = 64
GRID = 8
PAGES = 8
POS_BINS = 64
BOX_BINS = 32
PATCH = 64
TEXT = 512
PAIRS = HEADS // 2
LANES = 2 * HEAD
WINDOW = 144
SMALL = 80

dilation = 2
small_cost = pl.CostEstimate(flops=1000, bytes_accessed=1000, transcendentals=0)
norm_eps = 1e-05
mask_fill = -1000000000.0
erfc_poly = (
    0.2367515965428487,
    0.24062179898991767,
    0.18865103029313968,
    0.2877518531132804,
    -0.1648672439458568,
    0.4765735350541787,
    -0.34041833366480423,
    0.07493571514857543,
)
bf16 = jnp.bfloat16
f32 = jnp.float32


def shifted(values, offset, fill_value):
    padding = jnp.full((abs(offset),) + values.shape[1:], fill_value, values.dtype)
    if offset > 0:
        return jnp.concatenate([values[offset:], padding], axis=0)
    return jnp.concatenate([padding, values[:offset]], axis=0)


def dilated_mix(inputs, page_ids, conv_weight, conv_bias):
    summed = inputs + conv_bias + conv_weight[1] * inputs
    for tap_index, offset in ((0, -dilation), (2, dilation)):
        moved_rows = shifted(inputs, offset, 0.0)
        moved_pages = shifted(page_ids, offset, -1)
        same_page = (moved_pages == page_ids)[:, None]
        summed = summed + conv_weight[tap_index] * jnp.where(same_page, moved_rows, 0.0)
    return summed


def bin_features(pos_bins, bins_x, bins_y):
    return jnp.concatenate(
        [
            jax.nn.one_hot(pos_bins, POS_BINS, dtype=bf16),
            jax.nn.one_hot(bins_x, BOX_BINS, dtype=bf16),
            jax.nn.one_hot(bins_y, BOX_BINS, dtype=bf16),
        ],
        axis=1,
    )


def token_ids(text_pages, text_x, text_y):
    text_index = jnp.arange(TEXT, dtype=jnp.int32)
    text_pos = text_index * POS_BINS // TEXT
    patch_pos = text_index % PATCH * POS_BINS // PATCH
    patch_page = text_index // PATCH
    patch_x = text_index % GRID * BOX_BINS // GRID
    patch_y = text_index // GRID % GRID * BOX_BINS // GRID
    page_ids = jnp.stack([text_pages, patch_page])
    pos_bins = jnp.stack([text_pos, patch_pos])
    bins_x = jnp.stack([text_x, patch_x])
    bins_y = jnp.stack([text_y, patch_y])
    return (page_ids, pos_bins, bins_x, bins_y)


def plain_dot(left_side, right_side):
    return jnp.dot(left_side, right_side, preferred_element_type=f32)


def dot_left_t(left_side, right_side):
    return lax.dot_general(
        left_side, right_side, (((0,), (0,)), ((), ())), preferred_element_type=f32
    )


def dot_right_t(left_side, right_side):
    return lax.dot_general(
        left_side, right_side, (((1,), (1,)), ((), ())), preferred_element_type=f32
    )


def iota(shape, axis):
    return lax.broadcasted_iota(jnp.int32, shape, axis)


def bias_block(table_rows):
    pos_part = pltpu.roll(
        jnp.broadcast_to(table_rows[0:1], (POS_BINS, LANES)), 65, 1, stride=1, stride_axis=0
    )
    x_part = pltpu.roll(
        jnp.broadcast_to(table_rows[1:2], (BOX_BINS, LANES)), 33, 1, stride=1, stride_axis=0
    )
    y_part = pltpu.roll(
        jnp.broadcast_to(table_rows[2:3], (BOX_BINS, LANES)), 65, 1, stride=1, stride_axis=0
    )
    lane = iota((POS_BINS, LANES), 1)
    pos_part = jnp.where(lane < POS_BINS, pos_part, 0.0)
    lane = iota((BOX_BINS, LANES), 1)
    x_part = jnp.where((lane >= 64) & (lane < 96), x_part, 0.0)
    y_part = jnp.where(lane >= 96, y_part, 0.0)
    return jnp.concatenate([pos_part, x_part, y_part], axis=0).astype(bf16)


def diagonal_sums(grad_block):
    lane = iota((POS_BINS, LANES), 1)
    pos_part = jnp.where(lane < POS_BINS, grad_block[:64], 0.0)
    lane = iota((BOX_BINS, LANES), 1)
    x_part = jnp.where((lane >= 64) & (lane < 96), grad_block[64:96], 0.0)
    y_part = jnp.where(lane >= 96, grad_block[96:], 0.0)
    pos_part = pltpu.roll(pos_part, 0, 1, stride=1, stride_axis=0)
    x_part = pltpu.roll(x_part, 0, 1, stride=1, stride_axis=0)
    y_part = pltpu.roll(y_part, 96, 1, stride=1, stride_axis=0)
    rows = [jnp.sum(part, axis=0, keepdims=True) for part in (pos_part, x_part, y_part)]
    return jnp.concatenate(rows + [jnp.zeros((5, LANES), f32)], axis=0)


def stacked_heads(rows, low_lane):
    zero = jnp.zeros_like(rows)
    return jnp.concatenate(
        [jnp.where(low_lane, rows, zero), jnp.where(low_lane, zero, rows)], axis=0
    )


def window_start(first, window):
    return pl.multiple_of(jnp.minimum(first // 16 * 16, TEXT - window), 16)


def fits(first, end, window):
    return end - jnp.minimum(first // 16 * 16, TEXT - window) <= window


def for_each_page(bounds, step):
    def body(page, carry):
        own_low, own_high = bounds[page], bounds[PAGES + page]
        key_low, key_high = bounds[2 * PAGES + page], bounds[3 * PAGES + page]
        own_small = fits(own_low, own_high, SMALL)
        key_small = fits(key_low, key_high, SMALL)
        span = (own_low, own_high, key_low, key_high)
        small = own_small & key_small
        mixed = own_small & ~key_small
        for chosen, own_window, key_window in (
            (small, SMALL, SMALL),
            (mixed, SMALL, WINDOW),
            (~own_small, WINDOW, WINDOW),
        ):

            @pl.when(chosen)
            def _():
                step(page, span, own_window, key_window)

        return carry

    lax.fori_loop(0, PAGES, body, 0)


def page_operands(page, span, own_window, key_window, pair, q_ref, k_ref, feat_ref, lookup):
    own_at = window_start(span[0], own_window)
    key_at = window_start(span[2], key_window)
    own_rows, text_rows = pl.ds(own_at, own_window), pl.ds(key_at, key_window)
    patch_at = TEXT + PATCH * page
    if not isinstance(page, int):
        patch_at = pl.multiple_of(patch_at, PATCH)
    patch_rows = pl.ds(patch_at, PATCH)
    lanes = slice(pair * LANES, (pair + 1) * LANES)
    low_lane = iota((own_window, LANES), 1) < HEAD
    queries = stacked_heads(q_ref[own_rows, lanes], low_lane)
    first = 2 * pair * LANES
    rel = jnp.concatenate(
        [
            lookup[own_rows, first : first + LANES],
            lookup[own_rows, first + LANES : first + 2 * LANES],
        ],
        axis=0,
    )
    query_side = jnp.concatenate([rel, queries], axis=1)
    key_side = jnp.concatenate(
        [
            jnp.concatenate([feat_ref[text_rows, :], k_ref[text_rows, lanes]], axis=1),
            jnp.concatenate([feat_ref[patch_rows, :], k_ref[patch_rows, lanes]], axis=1),
        ],
        axis=0,
    )
    own_row = iota((own_window, LANES), 0) + own_at
    own_ok = (own_row >= span[0]) & (own_row < span[1])
    return (
        lanes, low_lane, own_ok, queries, query_side, key_side, own_rows, text_rows, patch_rows, key_at
    )


def set_lookup(lookup, own_feat_ref, table_ref):
    blocks = [bias_block(table_ref[head]) for head in range(table_ref.shape[0])]
    product = jnp.dot(
        own_feat_ref[...], jnp.concatenate(blocks, axis=1), preferred_element_type=f32
    )
    lookup[...] = product.astype(bf16)


def attend_kernel(bounds, q_ref, k_ref, v_ref, feat_ref, own_feat_ref, table_ref, context_ref, lookup):
    set_lookup(lookup, own_feat_ref, table_ref)

    def step(page, span, own_window, key_window):
        column = iota((1, key_window + PATCH), 1)
        key_row = column + window_start(span[2], key_window)
        key_ok = (column >= key_window) | ((key_row >= span[2]) & (key_row < span[3]))
        for pair in range(q_ref.shape[1] // LANES):
            lanes, low_lane, own_ok, _, query_side, key_side, own_rows, text_rows, patch_rows, _ = (
                page_operands(
                    page, span, own_window, key_window, pair, q_ref, k_ref, feat_ref, lookup
                )
            )
            scores = jnp.where(key_ok, dot_right_t(query_side, key_side), mask_fill)
            row_max = jnp.max(scores, axis=1, keepdims=True)
            weights = jnp.exp(scores - row_max)
            total = jnp.sum(weights, axis=1, keepdims=True)
            prob = (weights * (1.0 / total)).astype(bf16)
            values = jnp.concatenate([v_ref[text_rows, lanes], v_ref[patch_rows, lanes]], axis=0)
            mixed = jnp.dot(prob, values, preferred_element_type=f32)
            picked = jnp.where(low_lane, mixed[:own_window], mixed[own_window:])
            before = context_ref[own_rows, lanes].astype(f32)
            context_ref[own_rows, lanes] = jnp.where(own_ok, picked, before).astype(bf16)

    for page in range(PAGES):
        span = [bounds[part * PAGES + page] for part in range(4)]
        step(page, span, WINDOW, WINDOW)


def attend_back_kernel(
    bounds,
    q_ref,
    k_ref,
    v_ref,
    grad_ref,
    feat_ref,
    own_feat_ref,
    flip_feat_ref,
    table_ref,
    grad_q_ref,
    grad_k_ref,
    grad_v_ref,
    grad_table_ref,
    lookup,
    grad_lookup,
):
    set_lookup(lookup, own_feat_ref, table_ref)

    def step(page, span, own_window, key_window):
        row = iota((key_window + PATCH, 1), 0)
        key_row = row + window_start(span[2], key_window)
        key_ok = (row >= key_window) | ((key_row >= span[2]) & (key_row < span[3]))
        for pair in range(q_ref.shape[1] // LANES):
            lanes, low_lane, own_ok, queries, query_side, key_side, own_rows, text_rows, patch_rows, key_at = (
                page_operands(
                    page, span, own_window, key_window, pair, q_ref, k_ref, feat_ref, lookup
                )
            )
            scores = jnp.where(key_ok, dot_right_t(key_side, query_side), mask_fill)
            col_max = jnp.max(scores, axis=0, keepdims=True)
            weights = jnp.exp(scores - col_max)
            total = jnp.sum(weights, axis=0, keepdims=True)
            prob = weights * (1.0 / total)
            grad_rows = grad_ref[own_rows, lanes]
            grad_rows = jnp.where(own_ok, grad_rows, jnp.zeros_like(grad_rows))
            grads = stacked_heads(grad_rows, low_lane)
            values = jnp.concatenate([v_ref[text_rows, lanes], v_ref[patch_rows, lanes]], axis=0)
            grad_prob = dot_right_t(values, grads)
            inner = jnp.sum(prob * grad_prob, axis=0, keepdims=True)
            grad_scores = (prob * (grad_prob - inner)).astype(bf16)
            grad_v = jnp.dot(prob.astype(bf16), grads, preferred_element_type=f32)
            grad_k = jnp.dot(grad_scores, queries, preferred_element_type=f32)
            back = dot_left_t(grad_scores, key_side)
            low, high = back[:own_window], back[own_window:]
            grad_q = jnp.where(low_lane, low[:, LANES:], high[:, LANES:]) * 0.125
            before = grad_q_ref[own_rows, lanes].astype(f32)
            grad_q_ref[own_rows, lanes] = jnp.where(own_ok, grad_q, before).astype(bf16)
            first = 2 * pair * LANES
            for part, at in ((low, first), (high, first + LANES)):
                place_at = slice(at, at + LANES)
                grad_lookup[own_rows, place_at] = jnp.where(
                    own_ok, part[:, :LANES], grad_lookup[own_rows, place_at]
                )
            wide_row = iota((key_window, LANES), 0) + key_at
            text_ok = (wide_row >= span[2]) & (wide_row < span[3])
            for grad, ref in ((grad_k, grad_k_ref), (grad_v, grad_v_ref)):
                before = ref[text_rows, lanes].astype(f32)
                ref[text_rows, lanes] = jnp.where(text_ok, grad[:key_window], before).astype(bf16)
                ref[patch_rows, lanes] = grad[key_window:].astype(bf16)

    for_each_page(bounds, step)
    grad_high = grad_lookup[...].astype(bf16)
    grad_rest = (grad_lookup[...] - grad_high.astype(f32)).astype(bf16)
    flip = flip_feat_ref[...]
    grad_block = dot_left_t(flip, grad_high) + dot_left_t(flip, grad_rest)
    for head in range(table_ref.shape[0]):
        grad_table_ref[head] = diagonal_sums(grad_block[:, head * LANES : (head + 1) * LANES])


def column_spec(rows, group, first=0):
    return pl.BlockSpec((rows, group * LANES), lambda step, bounds: (0, step + first))


def whole_spec(rows):
    return pl.BlockSpec((rows, LANES), lambda step, bounds: (0, 0))


def tables_spec(group):
    return pl.BlockSpec((2 * group, 8, LANES), lambda step, bounds: (step, 0, 0))


def attend(bounds, queries, keys_values, features, own_features, tables):
    group = 1
    return pl.pallas_call(
        attend_kernel,
        grid_spec=pltpu.PrefetchScalarGridSpec(
            num_scalar_prefetch=1,
            grid=(PAIRS // group,),
            in_specs=[
                column_spec(TEXT, group),
                column_spec(2 * TEXT, group),
                column_spec(2 * TEXT, group, PAIRS // group),
                whole_spec(2 * TEXT),
                whole_spec(TEXT),
                tables_spec(group),
            ],
            out_specs=column_spec(TEXT, group),
            scratch_shapes=[pltpu.VMEM((TEXT, 2 * group * LANES), bf16)],
        ),
        out_shape=jax.ShapeDtypeStruct((TEXT, HEADS * HEAD), bf16),
        cost_estimate=small_cost,
        name="attend",
    )(bounds, queries, keys_values, keys_values, features, own_features, tables)


def attend_back(
    bounds, queries, keys_values, grad_context, features, own_features, flip, tables
):
    group = 6
    return pl.pallas_call(
        attend_back_kernel,
        grid_spec=pltpu.PrefetchScalarGridSpec(
            num_scalar_prefetch=1,
            grid=(PAIRS // group,),
            in_specs=[
                column_spec(TEXT, group),
                column_spec(2 * TEXT, group),
                column_spec(2 * TEXT, group, PAIRS // group),
                column_spec(TEXT, group),
                whole_spec(2 * TEXT),
                whole_spec(TEXT),
                whole_spec(TEXT),
                tables_spec(group),
            ],
            out_specs=[
                column_spec(TEXT, group),
                column_spec(2 * TEXT, group),
                column_spec(2 * TEXT, group),
                tables_spec(group),
            ],
            scratch_shapes=[
                pltpu.VMEM((TEXT, 2 * group * LANES), bf16),
                pltpu.VMEM((TEXT, 2 * group * LANES), f32),
            ],
        ),
        out_shape=[
            jax.ShapeDtypeStruct((TEXT, HEADS * HEAD), bf16),
            jax.ShapeDtypeStruct((2 * TEXT, HEADS * HEAD), bf16),
            jax.ShapeDtypeStruct((2 * TEXT, HEADS * HEAD), bf16),
            jax.ShapeDtypeStruct((HEADS, 8, LANES), f32),
        ],
        cost_estimate=small_cost,
        name="attend_back",
    )(
        bounds,
        queries,
        keys_values,
        keys_values,
        grad_context,
        features,
        own_features,
        flip,
        tables,
    )


def exchange(values, mask):
    count = lax.axis_size("page")
    return lax.ppermute(values, "page", [(i, i ^ mask) for i in range(count)])


def after(value, *earlier):
    return lax.optimization_barrier((value, *earlier))[0]


def slot_mask(slot):
    return (slot & 3) * 4 + (slot >> 2) * 2


def project_kernel(groups, place, mixed_ref, bias_ref, *refs):
    *pieces, query_ref, both_ref, weight_ref, mixed_t_ref, sems = refs
    width = mixed_ref.shape[1]
    tokens = query_ref.shape[0]
    copies = start_rows(place, groups, pieces, weight_ref, sems)
    mixed_t_ref[...] = mixed_ref[...].T
    for copy in copies:
        copy.wait()
    own = mixed_ref[pl.ds(pl.multiple_of(place[1] * tokens, 16), tokens), :]
    queries = jnp.dot(own, weight_ref[:, :width], preferred_element_type=f32) + bias_ref[:, :width]
    query_ref[...] = (queries.astype(bf16).astype(f32) * 0.125).astype(bf16)
    for part in range(2):
        rows = pl.ds(part * tokens, tokens)
        for column in (1, 2):
            at = slice(column * width, (column + 1) * width)
            out = slice((column - 1) * width, column * width)
            values = jnp.dot(mixed_ref[rows, :], weight_ref[:, at], preferred_element_type=f32)
            both_ref[rows, out] = (values + bias_ref[:, at]).astype(bf16)


def project(place, mixed, biases, groups, pieces):
    rows, width = mixed.shape
    vmem = pl.BlockSpec(memory_space=pltpu.VMEM)
    return pl.pallas_call(
        functools.partial(project_kernel, groups),
        grid_spec=pltpu.PrefetchScalarGridSpec(
            num_scalar_prefetch=1,
            grid=(),
            in_specs=[vmem] * 2 + any_specs(len(pieces)),
            out_specs=[vmem] * 4,
            scratch_shapes=[pltpu.SemaphoreType.DMA((32,))],
        ),
        out_shape=[
            jax.ShapeDtypeStruct((rows // 2, width), bf16),
            jax.ShapeDtypeStruct((rows, 2 * width), bf16),
            jax.ShapeDtypeStruct((width, 3 * width), bf16),
            jax.ShapeDtypeStruct((width, rows), bf16),
        ],
        cost_estimate=small_cost,
        compiler_params=pltpu.CompilerParams(vmem_limit_bytes=16 << 20),
        name="project",
    )(place, mixed, biases, *pieces)


def column_parts(shard):
    return [shard] + [exchange(shard, 4 * step) for step in (1, 2, 3)]


def half_pieces(column):
    eight = jnp.concatenate([column, exchange(column, 2)])
    far = swap(eight)
    return [eight, exchange(eight, 1), far, exchange(far, 1)]


def row_pieces(column, across):
    return [column, exchange(column, 1), across, exchange(across, 1)]


def column_of(shard):
    return jnp.stack(column_parts(shard))


def row_copies(place, groups, refs, full, sems, first=0):
    copies = []
    for kind, column in groups:
        if kind == "full":
            piece, *refs = refs
            width = piece.shape[1]
            target = full.at[:, pl.ds(column, width)]
            copies.append(pltpu.make_async_copy(piece, target, sems.at[first + len(copies)]))
            continue
        pieces, refs = refs[:4], refs[4:]
        _, rows, width = pieces[0].shape
        for index in range(32 if kind == "halves" else 16):
            at = column
            if kind == "halves":
                source, slot = index >> 3, index & 7
                mask = slot_mask(slot) + (source & 1)
                at = pl.multiple_of(column + (place[1] ^ (source >> 1)) * width, 128)
            else:
                source, slot = index & 3, index >> 2
                mask = slot * 4 + source
            row = pl.multiple_of((place[0] ^ mask) * rows, 16)
            copies.append(
                pltpu.make_async_copy(
                    pieces[source].at[slot],
                    full.at[pl.ds(row, rows), pl.ds(at, width)],
                    sems.at[first + len(copies)],
                )
            )
    return copies


def start_rows(place, groups, refs, full, sems):
    copies = row_copies(place, groups, refs, full, sems)
    for copy in copies:
        copy.start()
    return copies


def gelu_parts(values):
    size = jnp.abs(values)
    t = 1.0 / (1.0 + (0.42 * 0.7071067811865476) * size)
    poly = jnp.full_like(t, erfc_poly[-1])
    for coefficient in erfc_poly[-2::-1]:
        poly = poly * t + coefficient
    bell = jnp.exp(-0.5 * values * values)
    tail = (0.5 * t) * (poly * bell)
    cdf = jnp.where(values >= 0.0, 1.0 - tail, tail)
    return values * cdf, cdf + (values * 0.3989422804014327) * bell


def normalized(values):
    centered = values - jnp.mean(values, axis=1, keepdims=True)
    variance = jnp.mean(centered * centered, axis=1, keepdims=True)
    scale = lax.rsqrt(variance + norm_eps)
    return centered * scale, scale


def norm_back(grads, unit, scale, gain):
    scaled = grads * gain
    mean = jnp.mean(scaled, axis=1, keepdims=True)
    inner = jnp.mean(scaled * unit, axis=1, keepdims=True)
    return scale * (scaled - mean - unit * inner)


def up_kernel(groups, place, context_ref, mixed_ref, vec_ref, bias_ref, *refs):
    *pieces, unit_ref, scale_ref, low_ref, low_t_ref, context_t_ref = refs[:-9]
    active_ref, active_t_ref, slope_ref, full_ref = refs[-9:-5]
    weight, hidden, low, sems, full_sem = refs[-5:]
    step = pl.program_id(0)
    tiles = pl.num_programs(0) - 1
    width = context_ref.shape[1]
    tile = active_ref.shape[1]
    last_group = 16 if len(groups) > 1 else 0

    def full_copy():
        return pltpu.make_async_copy(weight, full_ref, full_sem)

    @pl.when(step == 0)
    def _():
        copies = row_copies(place, groups, pieces, weight, sems)
        for copy in copies:
            copy.start()
        context_t_ref[...] = context_ref[...].T
        for copy in copies[: len(copies) - last_group]:
            copy.wait()
        branch = jnp.dot(context_ref[...], weight[:, :width], preferred_element_type=f32)
        unit, scale = normalized(mixed_ref[...] + branch + vec_ref[0:1])
        unit_ref[...] = unit
        scale_ref[...] = jnp.broadcast_to(scale, scale_ref.shape)
        normed = (unit * vec_ref[1:2] + vec_ref[2:3]).astype(bf16)
        low[...] = normed
        low_ref[...] = normed
        low_t_ref[...] = normed.T

    @pl.when(step == 1)
    def _():
        if last_group:
            for copy in row_copies(place, groups[1:], pieces[4:], weight, sems, 32):
                copy.wait()
        full_copy().start()

    def product():
        at = pl.multiple_of(width + step * tile, 128)
        return jnp.dot(low[...], weight[:, pl.ds(at, tile)], preferred_element_type=f32)

    def activate():
        active, slope = gelu_parts(hidden[(step + 1) % 2] + bias_ref[...])
        active = active.astype(bf16)
        active_ref[...] = active
        active_t_ref[...] = active.T
        slope_ref[...] = slope.astype(bf16)

    @pl.when(step == 0)
    def _():
        hidden[step % 2] = product()

    @pl.when((step > 0) & (step < tiles))
    def _():
        hidden[step % 2] = product()
        activate()

    @pl.when(step == tiles)
    def _():
        activate()
        full_copy().wait()


def any_specs(count):
    return [pl.BlockSpec(memory_space=pl.ANY)] * count


def up_forward(place, context, mixed, vectors, bias_up, groups, pieces):
    tokens, width = mixed.shape
    hidden_width = bias_up.shape[1]
    tile = 512
    whole = lambda step, place: (0, 0)
    last = lambda step, place: (0, jnp.maximum(step - 1, 0))
    last_t = lambda step, place: (jnp.maximum(step - 1, 0), 0)
    return pl.pallas_call(
        functools.partial(up_kernel, groups),
        grid_spec=pltpu.PrefetchScalarGridSpec(
            num_scalar_prefetch=1,
            grid=(hidden_width // tile + 1,),
            in_specs=[
                pl.BlockSpec((tokens, width), whole),
                pl.BlockSpec((tokens, width), whole),
                pl.BlockSpec(vectors.shape, whole),
                pl.BlockSpec((1, tile), last),
            ]
            + any_specs(len(pieces)),
            out_specs=[
                pl.BlockSpec((tokens, width), whole),
                pl.BlockSpec((tokens, 128), whole),
                pl.BlockSpec((tokens, width), whole),
                pl.BlockSpec((width, tokens), whole),
                pl.BlockSpec((width, tokens), whole),
                pl.BlockSpec((tokens, tile), last),
                pl.BlockSpec((tile, tokens), last_t),
                pl.BlockSpec((tokens, tile), last),
                pl.BlockSpec(memory_space=pl.ANY),
            ],
            scratch_shapes=[
                pltpu.VMEM((width, width + hidden_width), bf16),
                pltpu.VMEM((2, tokens, tile), f32),
                pltpu.VMEM((tokens, width), bf16),
                pltpu.SemaphoreType.DMA((48,)),
                pltpu.SemaphoreType.DMA,
            ],
        ),
        out_shape=[
            jax.ShapeDtypeStruct((tokens, width), f32),
            jax.ShapeDtypeStruct((tokens, 128), f32),
            jax.ShapeDtypeStruct((tokens, width), bf16),
            jax.ShapeDtypeStruct((width, tokens), bf16),
            jax.ShapeDtypeStruct((width, tokens), bf16),
            jax.ShapeDtypeStruct((tokens, hidden_width), bf16),
            jax.ShapeDtypeStruct((hidden_width, tokens), bf16),
            jax.ShapeDtypeStruct((tokens, hidden_width), bf16),
            jax.ShapeDtypeStruct((width, width + hidden_width), bf16),
        ],
        cost_estimate=small_cost,
        name="up_forward",
    )(place, context, mixed, vectors, bias_up, *pieces)


def down_kernel(active_ref, weight_ref, unit_ref, vec_ref, grad_ref, *refs):
    out_ref, sum_ref, low_ref, small_ref, total = refs
    step = pl.program_id(0)
    product = jnp.dot(active_ref[...], weight_ref[...], preferred_element_type=f32)

    @pl.when(step == 0)
    def _():
        total[...] = product

    @pl.when(step > 0)
    def _():
        total[...] += product

    @pl.when(step == pl.num_programs(0) - 1)
    def _():
        tokens, width = unit_ref.shape
        half = tokens // 2
        smalls = [jnp.zeros((1, width), f32)] * 3
        for part in range(2):
            rows = pl.ds(part * half, half)
            normed = unit_ref[rows, :] * vec_ref[1:2] + vec_ref[2:3]
            unit, scale = normalized(normed + total[rows, :] + vec_ref[3:4])
            out_ref[rows, :] = (unit * vec_ref[4:5] + vec_ref[5:6]).astype(bf16)
            grads = grad_ref[rows, :].astype(f32)
            back = norm_back(grads, unit, scale, vec_ref[4:5])
            low = back.astype(bf16)
            sum_ref[rows, :] = back
            low_ref[rows, :] = low
            for index, term in enumerate((grads * unit, grads, low.astype(f32))):
                smalls[index] = smalls[index] + jnp.sum(term, axis=0, keepdims=True)
        small_ref[...] = jnp.concatenate(smalls + [jnp.zeros((5, width), f32)], axis=0)


def down_forward(active, weight, unit, vectors, grads):
    tokens, width = unit.shape
    hidden_width = active.shape[1]
    tile = 768
    whole = lambda step: (0, 0)
    token_block = pl.BlockSpec((tokens, width), whole)
    return pl.pallas_call(
        down_kernel,
        grid=(hidden_width // tile,),
        in_specs=[
            pl.BlockSpec((tokens, tile), lambda step: (0, step)),
            pl.BlockSpec((tile, width), lambda step: (step, 0)),
            token_block,
            pl.BlockSpec(vectors.shape, whole),
            token_block,
        ],
        out_specs=[token_block] * 3 + [pl.BlockSpec((8, width), whole)],
        scratch_shapes=[pltpu.VMEM((tokens, width), f32)],
        out_shape=[
            jax.ShapeDtypeStruct((tokens, width), bf16),
            jax.ShapeDtypeStruct((tokens, width), f32),
            jax.ShapeDtypeStruct((tokens, width), bf16),
            jax.ShapeDtypeStruct((8, width), f32),
        ],
        cost_estimate=small_cost,
        name="down_forward",
    )(active, weight, unit, vectors, grads)


def ffn_back_kernel(*refs):
    low_ref, slope_ref, sum_ref, unit_ref, scale_ref, vec_ref = refs[:6]
    down_ref, up_ref, out_weight_ref = refs[6:9]
    hidden_ref, bias_ref, first_ref, branch_ref, context_ref, small_ref, total = refs[9:]
    step = pl.program_id(0)
    tokens, width = unit_ref.shape
    tile = slope_ref.shape[1]
    half = tokens // 2

    @pl.when(step == 0)
    def _():
        total[...] = sum_ref[...]

    bias = jnp.zeros((1, tile), f32)
    for part in range(2):
        rows = pl.ds(part * half, half)
        grads = dot_right_t(low_ref[rows, :], down_ref[...]) * slope_ref[rows, :].astype(f32)
        grads = grads.astype(bf16)
        hidden_ref[rows, :] = grads
        bias = bias + jnp.sum(grads.astype(f32), axis=0, keepdims=True)
        total[rows, :] += dot_right_t(grads, up_ref[...])
    bias_ref[...] = bias

    @pl.when(step == pl.num_programs(0) - 1)
    def _():
        grads = total[...]
        unit = unit_ref[...]
        first = norm_back(grads, unit, scale_ref[:, 0:1], vec_ref[1:2])
        branch = first.astype(bf16)
        first_ref[...] = first
        branch_ref[...] = branch
        context_ref[...] = dot_right_t(branch, out_weight_ref[...]).astype(bf16)
        smalls = [
            jnp.sum(term, axis=0, keepdims=True)
            for term in (grads * unit, grads, branch.astype(f32))
        ]
        small_ref[...] = jnp.concatenate(smalls + [jnp.zeros((5, width), f32)], axis=0)


def ffn_back(low, slope, total, unit, scale, vectors, full_rest, full_down):
    tokens, width = unit.shape
    hidden_width = slope.shape[1]
    tile = 768
    whole = lambda step: (0, 0)
    column = lambda step: (0, step)
    token_block = pl.BlockSpec((tokens, width), whole)
    return pl.pallas_call(
        ffn_back_kernel,
        grid=(hidden_width // tile,),
        in_specs=[
            token_block,
            pl.BlockSpec((tokens, tile), column),
            token_block,
            token_block,
            pl.BlockSpec((tokens, 128), whole),
            pl.BlockSpec(vectors.shape, whole),
            pl.BlockSpec((tile, width), lambda step: (step, 0)),
            pl.BlockSpec((width, tile), lambda step: (0, step + 1)),
            pl.BlockSpec((width, width), whole),
        ],
        out_specs=[
            pl.BlockSpec((tokens, tile), column),
            pl.BlockSpec((1, tile), column),
            token_block,
            token_block,
            token_block,
            pl.BlockSpec((8, width), whole),
        ],
        scratch_shapes=[pltpu.VMEM((tokens, width), f32)],
        out_shape=[
            jax.ShapeDtypeStruct((tokens, hidden_width), bf16),
            jax.ShapeDtypeStruct((1, hidden_width), f32),
            jax.ShapeDtypeStruct((tokens, width), f32),
            jax.ShapeDtypeStruct((tokens, width), bf16),
            jax.ShapeDtypeStruct((tokens, width), bf16),
            jax.ShapeDtypeStruct((8, width), f32),
        ],
        cost_estimate=small_cost,
        name="ffn_back",
    )(low, slope, total, unit, scale, vectors, full_down, full_rest, full_rest)


def grad_rows_kernel(x_ref, h_ref, out_ref):
    out_ref[...] = jnp.dot(x_ref[...], h_ref[...], preferred_element_type=f32).astype(bf16)


def grad_rows(inputs_t, grads):
    width, tokens = inputs_t.shape
    columns = grads.shape[1]
    return pl.pallas_call(
        grad_rows_kernel,
        grid=(4,),
        in_specs=[
            pl.BlockSpec((width // 4, tokens), lambda step: (step, 0)),
            pl.BlockSpec((tokens, columns), lambda step: (0, 0)),
        ],
        out_specs=pl.BlockSpec((width // 4, columns), lambda step: (step, 0)),
        out_shape=jax.ShapeDtypeStruct((width, columns), bf16),
        cost_estimate=small_cost,
        name="grad_rows",
    )(inputs_t, grads)


def grad_columns_kernel(parts, place, *refs):
    count = len(parts)
    ins, keep_ref, send_ref, scratch = (
        refs[: 2 * count],
        refs[2 * count],
        refs[2 * count + 1],
        refs[2 * count + 2 :],
    )
    rows, tile = keep_ref.shape[1], keep_ref.shape[2]
    step = pl.program_id(0)
    first = 0
    for index, steps in enumerate(parts):
        x_ref, h_ref, ordered = ins[2 * index], ins[2 * index + 1], scratch[index]

        @pl.when(step == first)
        def _():
            for slot in range(16):
                mask = slot_mask(slot & 7) + (slot >> 3)
                at = pl.multiple_of((place[0] ^ mask) * rows, 16)
                ordered[pl.ds(slot * rows, rows), :] = x_ref[pl.ds(at, rows), :]

        @pl.when((step >= first) & (step < first + steps))
        def _():
            product = jnp.dot(ordered[...], h_ref[...], preferred_element_type=f32).astype(bf16)
            keep_ref[...] = product[: 8 * rows].reshape(8, rows, tile)
            send_ref[...] = product[8 * rows :].reshape(8, rows, tile)

        first = first + steps


def grad_by_columns(pairs, place, tile):
    width = pairs[0][0].shape[0]
    rows = width // 16
    parts = tuple(sum(grad.shape[1] for grad in grads) // tile for _, _, *grads in pairs)
    steps = sum(parts)
    specs = []
    operands = []
    scratch = []
    first = 0
    for (inputs_t, own, *grads), count in zip(pairs, parts):
        tokens = grads[0].shape[0]
        block = (lambda step, place: (0, place[1])) if own else (lambda step, place: (0, 0))
        specs.append(pl.BlockSpec((width, tokens), block))

        def column(step, place, first=first, count=count):
            return (0, jnp.clip(step - first, 0, count - 1))

        specs.append(pl.BlockSpec((tokens, tile), column))
        operands += [inputs_t, *grads]
        scratch.append(pltpu.VMEM((width, tokens), bf16))
        first = first + count
    half = jax.ShapeDtypeStruct((8, rows, steps * tile), bf16)
    return pl.pallas_call(
        functools.partial(grad_columns_kernel, parts),
        grid_spec=pltpu.PrefetchScalarGridSpec(
            num_scalar_prefetch=1,
            grid=(steps,),
            in_specs=specs,
            out_specs=[pl.BlockSpec((8, rows, tile), lambda step, place: (0, 0, step))] * 2,
            scratch_shapes=scratch,
        ),
        out_shape=[half, half],
        cost_estimate=small_cost,
        compiler_params=pltpu.CompilerParams(vmem_limit_bytes=16 << 20),
        name="grad_columns",
    )(place, *operands)


def key_back_kernel(place, gk_ref, gv_ref, wk_ref, wv_ref, out_ref):
    total = dot_right_t(gk_ref[...], wk_ref[...]) + dot_right_t(gv_ref[...], wv_ref[...])
    out_ref[...] = total.astype(out_ref.dtype)


def own_back_kernel(place, first_ref, gq_ref, gk_ref, gv_ref, wq_ref, wk_ref, wv_ref, out_ref):
    total = dot_right_t(gk_ref[...], wk_ref[...]) + dot_right_t(gv_ref[...], wv_ref[...])
    out_ref[...] = first_ref[...] + total + dot_right_t(gq_ref[...], wq_ref[...])


def input_back(place, weights, grad_keys, grad_values, others):
    width = weights.shape[0]
    tokens = grad_keys.shape[0] // 2
    whole = pl.BlockSpec((tokens, width), lambda step, place: (0, 0))
    row = lambda step, place: ((place[1] if others else 1 - place[1]), 0)
    if others:
        kernel, leading, first, dtype = own_back_kernel, [whole, whole], 0, f32
    else:
        kernel, leading, first, dtype = key_back_kernel, [], 1, bf16
    operands = list(others) + [grad_keys, grad_values] + [weights] * (3 - first)
    specs = [pl.BlockSpec((tokens, width), row)] * 2
    for block in range(first, 3):
        specs.append(pl.BlockSpec((width, width), lambda step, place, block=block: (0, block)))
    return pl.pallas_call(
        kernel,
        grid_spec=pltpu.PrefetchScalarGridSpec(
            num_scalar_prefetch=1, grid=(1,), in_specs=leading + specs, out_specs=whole
        ),
        out_shape=jax.ShapeDtypeStruct((tokens, width), dtype),
        cost_estimate=small_cost,
        compiler_params=pltpu.CompilerParams(vmem_limit_bytes=16 << 20),
        name="input_back",
    )(place, *operands)


def back_rows(values, mask):
    return jnp.where(mask, pltpu.roll(values, dilation, 0), 0.0)


def ahead_rows(values, mask):
    return jnp.where(mask, pltpu.roll(values, values.shape[0] - dilation, 0), 0.0)


def tap_sums(grads, inputs, ahead, back):
    terms = (grads * back_rows(inputs, back), grads * inputs, grads * ahead_rows(inputs, ahead), grads)
    return [jnp.sum(term, axis=0, keepdims=True) for term in terms]


def small_sums_kernel(
    own_ref, other_ref, x_ref, x_other_ref, mask_ref, gq_ref, gv_ref, one_ref, two_ref, up_ref, table_ref, out_ref
):
    width = own_ref.shape[1]
    mask = mask_ref[...] > 0.0
    own = tap_sums(own_ref[...], x_ref[...].astype(f32), mask[:, 0:1], mask[:, 1:2])
    other = tap_sums(
        other_ref[...].astype(f32), x_other_ref[...].astype(f32), mask[:, 2:3], mask[:, 3:4]
    )
    rows = [a + b for a, b in zip(own, other)]
    for ref in (gq_ref, gv_ref):
        rows.append(jnp.sum(ref[...].astype(f32), axis=0, keepdims=True))
    rows.append(jnp.zeros((2, width), f32))
    out_ref[0:8] = jnp.concatenate(rows, axis=0)
    out_ref[8:16] = one_ref[...]
    out_ref[16:24] = two_ref[...]
    count = up_ref.shape[1] // width
    for index in range(count):
        out_ref[24 + index : 25 + index] = up_ref[:, index * width : (index + 1) * width]
    for index in range(3 * HEADS):
        row, lane = 28 + index // 6, index % 6 * LANES
        table = table_ref[index // 3]
        out_ref[row : row + 1, lane : lane + LANES] = table[index % 3 : index % 3 + 1]
    out_ref[34:40] = jnp.zeros((6, width), f32)


def small_sums(*operands):
    return pl.pallas_call(
        small_sums_kernel,
        out_shape=jax.ShapeDtypeStruct((40, operands[0].shape[1]), f32),
        cost_estimate=small_cost,
        compiler_params=pltpu.CompilerParams(vmem_limit_bytes=24 << 20),
        name="small_sums",
    )(*operands)


def state_back_kernel(own_ref, other_ref, mask_ref, tap_ref, out_ref):
    grads = own_ref[...] + other_ref[...].astype(f32)
    mask = mask_ref[...] > 0.0
    total = grads + tap_ref[1:2] * grads
    total = total + tap_ref[0:1] * ahead_rows(grads, mask[:, 0:1])
    total = total + tap_ref[2:3] * back_rows(grads, mask[:, 1:2])
    out_ref[...] = total.astype(bf16)


def state_back(own, other, masks, taps):
    return pl.pallas_call(
        state_back_kernel,
        out_shape=jax.ShapeDtypeStruct(own.shape, bf16),
        cost_estimate=small_cost,
        compiler_params=pltpu.CompilerParams(vmem_limit_bytes=20 << 20),
        name="state_back",
    )(own, other, masks, taps)


def first_half_kernel(place, keep_near, part_near, keep_far, part_far, held_ref, out_ref):
    held_ref[...] = keep_near[...].astype(f32) + part_near[...].astype(f32)
    out_ref[...] = (keep_far[...].astype(f32) + part_far[...].astype(f32)).astype(bf16)


def halve_call(place, keep, partner, specs, half_shape, steps):
    near, far, out = specs
    return pl.pallas_call(
        first_half_kernel,
        grid_spec=pltpu.PrefetchScalarGridSpec(
            num_scalar_prefetch=1,
            grid=(steps,),
            in_specs=[near, near, far, far],
            out_specs=[out, out],
        ),
        out_shape=[
            jax.ShapeDtypeStruct(half_shape, f32),
            jax.ShapeDtypeStruct(half_shape, bf16),
        ],
        cost_estimate=small_cost,
        compiler_params=pltpu.CompilerParams(vmem_limit_bytes=12 << 20),
        name="halve",
    )(place, keep, partner, keep, partner)


def halve_across(place, keep, partner):
    _, rows, width = keep.shape
    near = pl.BlockSpec((1, rows, width), lambda step, place: (step, 0, 0))
    far = pl.BlockSpec((1, rows, width), lambda step, place: (step + 4, 0, 0))
    return halve_call(place, keep, partner, (near, far, near), (4, rows, width), 4)


def halve_plane(place, keep, partner):
    _, rows, width = keep.shape
    block = (2, rows, width // 2)
    near = pl.BlockSpec(block, lambda step, place: (step, 0, place[1]))
    far = pl.BlockSpec(block, lambda step, place: (step, 0, 1 - place[1]))
    out = pl.BlockSpec(block, lambda step, place: (step, 0, 0))
    return halve_call(place, keep, partner, (near, far, out), (8, rows, width // 2), 4)


def column_kernel(held_ref, across_ref, own_ref, *sends):
    own_ref[...] = held_ref[0] + across_ref[0].astype(f32)
    for step, send in enumerate(sends, 1):
        send[...] = (held_ref[step] + across_ref[step].astype(f32)).astype(bf16)


def column_sends(held, across):
    _, rows, width = held.shape
    tile = 384
    out = pl.BlockSpec((rows, tile), lambda step: (0, step))
    block = pl.BlockSpec((4, rows, tile), lambda step: (0, 0, step))
    own, *sends = pl.pallas_call(
        column_kernel,
        grid=(width // tile,),
        in_specs=[block, block],
        out_specs=[out] * 4,
        out_shape=[jax.ShapeDtypeStruct((rows, width), f32)]
        + [jax.ShapeDtypeStruct((rows, width), bf16)] * 3,
        cost_estimate=small_cost,
        compiler_params=pltpu.CompilerParams(vmem_limit_bytes=12 << 20),
        name="column_sends",
    )(held, across)
    return own, sends


def column_arrivals(sends):
    return [exchange(send, 4 * step) for step, send in enumerate(sends, 1)]


def column_total(own, arrived):
    total = own
    for part in arrived:
        total = total + part.astype(f32)
    return total.astype(bf16)


def half_columns(values, first):
    half = values.shape[-1] // 2
    return jnp.where(first, values[..., :half], values[..., half:])


def summed_rows(pairs):
    grads = jnp.concatenate([plain_dot(*pair).astype(bf16) for pair in pairs], axis=1)
    shard = lax.psum_scatter(grads, "page", scatter_dimension=0, tiled=True)
    return shard.astype(f32) + swap(shard).astype(f32)


def page_bounds(segments, is_text):
    pages = jnp.arange(PAGES, dtype=jnp.int32)
    low = jnp.sum(segments[None, :] < pages[:, None], axis=1, dtype=jnp.int32)
    high = jnp.sum(segments[None, :] <= pages[:, None], axis=1, dtype=jnp.int32)
    own_low = jnp.where(is_text, low, pages * PATCH)
    own_high = jnp.where(is_text, high, (pages + 1) * PATCH)

    return jnp.concatenate([own_low, own_high, low, high])


def both_sum(values, mask):
    return values + exchange(values, mask)


def swap(values):
    return lax.ppermute(values, "mod", [(0, 1), (1, 0)])


def local(
    states,
    cotangent,
    segments,
    box_x,
    box_y,
    conv_weight,
    conv_bias,
    w_query,
    b_query,
    w_key,
    w_value,
    b_value,
    w_out,
    b_out,
    table_pos,
    table_x,
    table_y,
    gain_one,
    bias_one,
    w_up,
    b_up,
    w_down,
    b_down,
    gain_two,
    bias_two,
):
    is_text = lax.axis_index("mod") == 0
    d_model = states.shape[3]
    own_low = states[0, 0]
    rows_each = w_query.shape[0]
    d_ff = w_up.shape[1]
    fast = lax.axis_size("page") == 16 and rows_each % 16 == 0 and w_down.shape[0] % 16 == 0
    place = jnp.stack([lax.axis_index("page"), lax.axis_index("mod")]).astype(jnp.int32)
    pack_qkv = jnp.concatenate([w_query, w_key, w_value], axis=1)
    pack_rest = jnp.concatenate([w_out, w_up], axis=1)
    other_low = swap(own_low)
    page_ids, pos_bins, bins_x, bins_y = token_ids(segments[0], box_x[0], box_y[0])
    bounds = page_bounds(segments[0], is_text)
    own_pages = jnp.where(is_text, page_ids[0], page_ids[1])
    features = bin_features(pos_bins.reshape(-1), bins_x.reshape(-1), bins_y.reshape(-1))
    flipped = bin_features(
        POS_BINS - 1 - pos_bins.reshape(-1),
        BOX_BINS - 1 - bins_x.reshape(-1),
        BOX_BINS - 1 - bins_y.reshape(-1),
    )
    own_feats = jnp.where(is_text, features[:TEXT], features[TEXT:])
    own_flip = jnp.where(is_text, flipped[:TEXT], flipped[TEXT:])
    tables = jnp.stack(
        [
            jnp.pad(table_pos, ((0, 0), (0, LANES - table_pos.shape[1]))),
            jnp.pad(table_x, ((0, 0), (0, LANES - table_x.shape[1]))),
            jnp.pad(table_y, ((0, 0), (0, LANES - table_y.shape[1]))),
        ],
        axis=1,
    )
    tables = jnp.pad(tables, ((0, 0), (0, 5), (0, 0)))

    own_states = own_low.astype(f32)
    mixed = dilated_mix(own_states, own_pages, conv_weight, conv_bias)
    mixed_low = mixed.astype(bf16)
    other_pages = jnp.where(is_text, page_ids[1], page_ids[0])
    masks = jnp.pad(
        jnp.stack(
            [
                own_pages == shifted(own_pages, dilation, -1),
                own_pages == shifted(own_pages, -dilation, -1),
                other_pages == shifted(other_pages, dilation, -1),
                other_pages == shifted(other_pages, -dilation, -1),
            ],
            axis=1,
        ).astype(f32),
        ((0, 0), (0, LANES - 4)),
    )
    vectors = jnp.stack(
        [b_out, gain_one, bias_one, b_down, gain_two, bias_two, jnp.zeros_like(b_out), b_out]
    )
    biases = jnp.concatenate([b_query, jnp.zeros_like(b_value), b_value])[None]
    taps = jnp.pad(conv_weight, ((0, 5), (0, 0)))
    bias_up = b_up[None]
    if fast:
        split = (pack_rest.shape[1] // 2 + 127) // 256 * 256
        column_qkv = column_of(half_columns(pack_qkv, is_text))
        early = (features, own_feats, own_flip, tables, bounds, masks, vectors, biases, taps)
        parts_near = column_parts(after(half_columns(pack_rest[:, :split], is_text), column_qkv))
        w_down = after(w_down, column_qkv)
        pieces_qkv = half_pieces(column_qkv)
        column_near = jnp.stack([after(part, pieces_qkv[0]) for part in parts_near])
        parts_far = column_parts(after(pack_rest[:, split:], column_near))
        pieces_near = half_pieces(column_near)
        pieces_qkv[2] = after(pieces_qkv[2], pieces_near[0])
        pieces_qkv[3] = exchange(pieces_qkv[2], 1)
        groups_qkv = (("halves", 0),)
    else:
        groups_qkv = (("full", 0),)
        pieces_qkv = [lax.all_gather(pack_qkv, "page", axis=0, tiled=True)]
    full_down = lax.all_gather(w_down, "page", axis=0, tiled=True)

    other_mixed = dilated_mix(other_low.astype(f32), other_pages, conv_weight, conv_bias)
    other_mixed = other_mixed.astype(bf16)
    mixed_all = jnp.concatenate(
        [jnp.where(is_text, mixed_low, other_mixed), jnp.where(is_text, other_mixed, mixed_low)],
        axis=0,
    )
    if fast:
        pieces_qkv[0] = after(pieces_qkv[0], mixed_all, bias_up, *early)
    queries, keys_values, full_qkv, mixed_t = project(
        place, mixed_all, biases, groups_qkv, pieces_qkv
    )
    attend_in = queries
    if fast:
        column_far = jnp.stack([after(part, queries) for part in parts_far])
        across_far = exchange(column_far, 2)
        attend_in = after(queries, column_far)
    context = attend(bounds, attend_in, keys_values, features, own_feats, tables)
    if fast:
        pieces_near[2] = after(pieces_near[2], context)
        pieces_near[3] = exchange(pieces_near[2], 1)
        across_far = after(across_far, context)
        pieces_rest = pieces_near + row_pieces(column_far, across_far)
        groups_rest = (("halves", 0), ("rows", split))
    else:
        pieces_rest = [lax.all_gather(pack_rest, "page", axis=0, tiled=True)]
        groups_rest = (("full", 0),)
    unit, scale, normed_low, normed_t, context_t, active, active_t, slope, full_rest = up_forward(
        place, context, mixed, vectors, bias_up, groups_rest, pieces_rest
    )
    output_row, grad_sum_two, grad_ffn, small_two = down_forward(
        active, full_down, unit, vectors, cotangent[0, 0]
    )
    rows_down = grad_rows(active_t, grad_ffn)
    shard_down = lax.psum_scatter(rows_down, "page", scatter_dimension=0, tiled=True)
    grad_hidden, grad_b_up, grad_first, grad_branch, grad_context, small_one = ffn_back(
        after(grad_ffn, rows_down), slope, grad_sum_two, unit, scale, vectors, full_rest, full_down
    )
    attend_in = grad_context
    if fast:
        pairs = [(context_t, False, grad_branch), (normed_t, False, grad_hidden)]
        keep_rest, send_rest = grad_by_columns(pairs, place, d_model)
        partner_rest = exchange(send_rest, 1)
        held_rest, plane_out = halve_plane(place, keep_rest, partner_rest)
        plane_rest = swap(plane_out)
        attend_in = after(grad_context, plane_out)
    else:
        shard_rest = summed_rows([(context_t, grad_branch), (normed_t, grad_hidden)])
    grad_queries, grad_keys, grad_values, grad_tables = attend_back(
        bounds, queries, keys_values, attend_in, features, own_feats, own_flip, tables
    )
    grad_keys_in, grad_queries_in = grad_keys, grad_queries
    if fast:
        plane_rest = after(plane_rest, grad_queries)
        held_rest, across_out = halve_across(place, held_rest, plane_rest)
        across_rest = exchange(across_out, 2)
        grad_queries_in = after(grad_queries, across_out)
    pairs = [(mixed_t, True, grad_queries_in), (mixed_t, False, grad_keys), (mixed_t, False, grad_values)]
    if fast:
        keep_qkv, send_qkv = grad_by_columns(pairs, place, d_model)
        partner_qkv = exchange(send_qkv, 1)
        grad_keys_in = after(grad_keys, send_qkv)
    else:
        shard_down = shard_down.astype(f32) + swap(shard_down).astype(f32)
        shard_qkv = summed_rows(
            [(mixed_low.T, grad_queries), (mixed_t, grad_keys), (mixed_t, grad_values)]
        )
    to_other = input_back(place, full_qkv, grad_keys_in, grad_values, ())
    from_other = swap(to_other)
    grad_values_in = grad_values
    if fast:
        partner_qkv = after(partner_qkv, to_other)
        held_qkv, across_out = halve_across(place, keep_qkv, partner_qkv)
        across_qkv = exchange(across_out, 2)
        grad_values_in = after(grad_values, across_out)
    own_part = input_back(place, full_qkv, grad_keys, grad_values_in, (grad_first, grad_queries))
    packed = small_sums(
        own_part,
        to_other,
        own_low,
        other_low,
        masks,
        grad_queries,
        grad_values,
        small_one,
        small_two,
        grad_b_up,
        grad_tables,
    )
    if fast:
        packed = both_sum(packed, 1)
        shard_down = after(shard_down, packed)
        across_rest = after(across_rest, packed, shard_down)
        shard_down = shard_down.astype(f32) + swap(shard_down).astype(f32)
        own_rest, sends_rest = column_sends(held_rest, across_rest)
        arrived_rest = column_arrivals(sends_rest)
        packed = after(packed, *sends_rest)
        packed = packed + swap(packed)
        across_qkv = after(across_qkv, packed)
        own_qkv, sends_qkv = column_sends(held_qkv, across_qkv)
        arrived_qkv = column_arrivals(sends_qkv)
        from_other = after(from_other, *sends_qkv)
    else:
        packed = lax.psum(packed, ("mod", "page"))
    grad_in = state_back(own_part, from_other, masks, taps)
    if fast:
        arrived_rest = [after(part, grad_in) for part in arrived_rest]
        total_rest = column_total(own_rest, arrived_rest)
        far_rest = swap(total_rest)
        packed = both_sum(after(packed, total_rest), 2)
        arrived_qkv = [after(part, packed) for part in arrived_qkv]
        total_qkv = column_total(own_qkv, arrived_qkv)
        far_qkv = swap(total_qkv)
        packed = both_sum(both_sum(after(packed, total_qkv), 4), 8)
    g_tables = packed[28:34].reshape(HEADS, 3, LANES)
    if fast:
        shard_rest = jnp.where(
            is_text,
            jnp.concatenate([total_rest, far_rest], axis=1),
            jnp.concatenate([far_rest, total_rest], axis=1),
        ).astype(f32)
        shard_qkv = total_qkv.astype(f32) + far_qkv.astype(f32)
    return (
        output_row[None, None],
        grad_in[None, None],
        packed[0:3],
        packed[3],
        shard_qkv[:, :d_model],
        packed[4],
        shard_qkv[:, d_model : 2 * d_model],
        shard_qkv[:, 2 * d_model :],
        packed[5],
        shard_rest[:, :d_model],
        packed[10],
        g_tables[:, 0, : table_pos.shape[1]],
        g_tables[:, 1, 64 : 64 + table_x.shape[1]],
        g_tables[:, 2, 64 : 64 + table_y.shape[1]],
        packed[8],
        packed[9],
        shard_rest[:, d_model:],
        packed[24:28].reshape(d_ff),
        shard_down,
        packed[18],
        packed[16],
        packed[17],
    )


def solution(mesh):
    rows = P("mod", "page", None, None)
    ids = P("page", None)
    cut = P("page", None)
    return jax.shard_map(
        local,
        mesh=mesh,
        in_specs=(
            rows, rows, ids, ids, ids, P(), P(), cut, P(), cut, cut, P(), cut,
            P(), P(), P(), P(), P(), P(), cut, P(), cut, P(), P(), P(),
        ),
        out_specs=(
            rows, rows, P(), P(), cut, P(), cut, cut, P(), cut, P(), P(), P(),
            P(), P(), P(), cut, P(), cut, P(), P(), P(),
        ),
        check_vma=False,
    )
```

profile of v0, /device:TPU:0, one launch (start us, length us, event | category | flops | bytes accessed | tf_op | source)
XLA Modules:
  0.0 328.2 jit_solution(644827435596206523)
XLA Ops:
  8.2 3.1 collective-permute-start.1
  11.3 2.6 collective-permute-start.2
  41.3 3.5 %collective-permute-start.8 = (bf16[48,896]{1,0:T(8,128)(2,1)S(1)}, bf16[48,896]{1,0:T(8,128)(2,1)S(1)}, u32[]{:S(2)}, u32[]{:S(2)}) collective-permute-start(bf16[48,896]{1,0:T(8,128)(2,1)S(1)} %fusion.2), channel_id=1, source_target_pairs={{0,8},{1,9},{2,10},{3,11},{4,12},{5,13},{6,14},{7,15},{8,0},{9,1},... | collective-permute-start | bytes 258056 | tf_op jit(solution)/shard_map/ppermute | solution.py:404
  45.1 8.0 %collective-permute-done.4 = bf16[4,48,1152]{2,1,0:T(8,128)(2,1)S(1)} collective-permute-done((bf16[4,48,1152]{2,1,0:T(8,128)(2,1)S(1)}, bf16[4,48,1152]{2,1,0:T(8,128)(2,1)S(1)}, u32[]{:S(2)}, u32[]{:S(2)}) %collective-permute-start.4) | collective-permute-done | bytes 442400 | tf_op jit(solution)/shard_map/ppermute | solution.py:404
  58.1 3.0 collective-permute-start.12
  61.1 2.4 collective-permute-start.13
  65.0 3.5 %collective-permute-start.14 = (bf16[48,2048]{1,0:T(8,128)(2,1)}, bf16[48,2048]{1,0:T(8,128)(2,1)S(1)}, u32[]{:S(2)}, u32[]{:S(2)}) collective-permute-start(bf16[48,2048]{1,0:T(8,128)(2,1)} %slice.152), channel_id=1, source_target_pairs={{0,12},{1,13},{2,14},{3,15},{4,8},{5,9},{6,10},{7,11},{8,4},{9,5},... | collective-permute-start | bytes 589832 | tf_op jit(solution)/shard_map/ppermute | solution.py:404
  69.3 2.0 collective-permute-done.6.refs_2_
  71.4 2.1 broadcast_select_fusion.1
  75.9 5.5 %project.1 = (bf16[512,768]{1,0:T(8,128)(2,1)S(1)}, bf16[1024,1536]{1,0:T(8,128)(2,1)S(1)}, bf16[768,2304]{1,0:T(8,128)(2,1)S(1)}, bf16[768,1024]{1,0:T(8,128)(2,1)S(1)}) custom-call(s32[2]{0:T(128)S(1)} %pad_add_fusion.1.place, bf16[1024,768]{1,0:T(8,128)(2,1)S(1)} %pad_maximum_fusion.mixed_ref, f32[1,2304]{1,0:T(1,128)S(1)} %broadcast_in_dim.67.bias_ref, ...), custom_call_target="tpu_custom_call" | custom-call | flops 1000 | bytes 1000 | tf_op jit(solution)/shard_map/project/pallas_call | solution.py:438
  85.2 1.7 collective-permute-done.13
  86.9 1.9 pad_maximum_fusion.1.refs_4_
  90.0 12.9 %attend.1.context_ref = bf16[512,768]{1,0:T(8,128)(2,1)} custom-call(s32[32]{0:T(128)} %pad_add_fusion.2.bounds, bf16[512,768]{1,0:T(8,128)(2,1)} %copy-done.14, bf16[1024,1536]{1,0:T(8,128)(2,1)} %copy-done, bf16[1024,1536]{1,0:T(8,128)(2,1)} %copy-done, bf16[1024,128]{1,0:T(8,128)(2,1)} %copy-done.36, bf16[512,128]{1,0:T(8,128)(2,1)} %slice_select_fusion.1.own_feat_ref, ...), custom_call_target="tpu_custom_call" | custom-call | flops 1000 | bytes 1000 | tf_op jit(solution)/shard_map/attend/pallas_call | solution.py:329
  102.9 5.3 %collective-permute-done.19.refs_6_ = bf16[4,48,2048]{2,1,0:T(8,128)(2,1)} collective-permute-done((bf16[4,48,2048]{2,1,0:T(8,128)(2,1)}, bf16[4,48,2048]{2,1,0:T(8,128)(2,1)}, u32[]{:S(2)}, u32[]{:S(2)}) %collective-permute-start.19) | collective-permute-done | bytes 786464 | tf_op jit(solution)/shard_map/ppermute | solution.py:404
  108.8 3.1 collective-permute-done.15.refs_1_
  112.8 19.6 %up_forward.1 = (f32[512,768]{1,0:T(8,128)}, f32[512,128]{1,0:T(8,128)}, bf16[512,768]{1,0:T(8,128)(2,1)}, bf16[768,512]{1,0:T(8,128)(2,1)}, bf16[768,512]{1,0:T...) custom-call(s32[2]{0:T(128)} %copy-done.30, ...), custom_call_target="tpu_custom_call" | custom-call | flops 1000 | bytes 1000 | tf_op jit(solution)/shard_map/up_forward/pallas_call | solution.py:615
  132.4 10.1 %down_forward.1 = (bf16[512,768]{1,0:T(8,128)(2,1)}, f32[512,768]{1,0:T(8,128)}, bf16[512,768]{1,0:T(8,128)(2,1)}, f32[8,768]{1,0:T(8,128)}) custom-call(bf16[512,3072]{1,0:T(8,128)(2,1)} %get-tuple-element.119.active_ref, bf16[3072,768]{1,0:T(8,128)(2,1)} %all-gather.2.cloned.1.call-done.weight_ref.refs_6_, f32[512,768]{1,0:T(8,128)} %get-tuple-element.121.unit_ref.refs_3_, ...), custom_call_target="tpu_custom_call" | custom-call | flops 1000 | bytes 1000 | tf_op jit(solution)/shard_map/down_forward/pallas_call | solution.py:701
  142.5 6.4 %grad_rows.1 = bf16[3072,768]{1,0:T(8,128)(2,1)} custom-call(bf16[3072,512]{1,0:T(8,128)(2,1)} %get-tuple-element.124.x_ref, bf16[512,768]{1,0:T(8,128)(2,1)} %get-tuple-element.125.h_ref.refs_0_), custom_call_target="tpu_custom_call" | custom-call | flops 1000 | bytes 1000 | tf_op jit(solution)/shard_map/grad_rows/pallas_call | solution.py:813
  149.0 14.5 %ffn_back.1 = (bf16[512,3072]{1,0:T(8,128)(2,1)}, f32[1,3072]{1,0:T(1,128)}, f32[512,768]{1,0:T(8,128)}, bf16[512,768]{1,0:T(8,128)(2,1)}, bf16[512,768]{1,0:T(8,128)(2,1)}, /*index=5*/f32[8,768]{1,0:T(8,128)}) custom-call(bf16[512,768]{1,0:T(8,128)(2,1)} %get-tuple-element.125.h_ref.refs_0_, bf16[512,3072]{1,0:T(8,128)(2,1)} %get-tuple-element.126.refs_1_, ...), custom_call_target="tpu_custom_call" | custom-call | flops 1000 | bytes 1000 | tf_op jit(solution)/shard_map/ffn_back/pallas_call | solution.py:770
  163.5 2.1 copy-done.15
  169.1 5.4 %grad_columns.2 = (bf16[8,48,3840]{2,1,0:T(8,128)(2,1)S(1)}, bf16[8,48,3840]{2,1,0:T(8,128)(2,1)S(1)}) custom-call(s32[2]{0:T(128)S(1)} %copy-done.31, bf16[768,512]{1,0:T(8,128)(2,1)S(1)} %copy-done.26, bf16[512,768]{1,0:T(8,128)(2,1)S(1)} %copy-done.27, bf16[768,512]{1,0:T(8,128)(2,1)S(1)} %copy-done.25, bf16[512,3072]{1,0:T(8,128)(2,1)S(1)} %copy-done.15), custom_call_target="tpu_custom_call" | custom-call | flops 1000 | bytes 1000 | tf_op jit(solution)/shard_map/grad_columns/pallas_call | solution.py:879
  174.6 5.3 %collective-permute-done.21.part_near.part_far = bf16[8,48,3840]{2,1,0:T(8,128)(2,1)S(1)} collective-permute-done((bf16[8,48,3840]{2,1,0:T(8,128)(2,1)S(1)}, bf16[8,48,3840]{2,1,0:T(8,128)(2,1)S(1)}, u32[]{:S(2)}, u32[]{:S(2)}) %collective-permute-start.21) | collective-permute-done | bytes 2949152 | tf_op jit(solution)/shard_map/ppermute | solution.py:404
  179.9 3.0 halve.3
  184.8 24.6 %attend_back.1 = (bf16[512,768]{1,0:T(8,128)(2,1)}, bf16[1024,768]{1,0:T(8,128)(2,1)}, bf16[1024,768]{1,0:T(8,128)(2,1)}, f32[12,8,128]{2,1,0:T(8,128)}) custom-call(s32[32]{0:T(128)} %pad_add_fusion.2.bounds, bf16[512,768]{1,0:T(8,128)(2,1)} %copy-done.14, bf16[1024,1536]{1,0:T(8,128)(2,1)} %copy-done, bf16[1024,1536]{1,0:T(8,128)(2,1)} %copy-done, ...), custom_call_target="tpu_custom_call" | custom-call | flops 1000 | bytes 1000 | tf_op jit(solution)/shard_map/attend_back/pallas_call | solution.py:355
  209.4 9.6 %collective-permute-done.22.part_near.part_far = bf16[8,48,1920]{2,1,0:T(8,128)(2,1)} collective-permute-done((bf16[8,48,1920]{2,1,0:T(8,128)(2,1)}, bf16[8,48,1920]{2,1,0:T(8,128)(2,1)}, u32[]{:S(2)}, u32[]{:S(2)}) %collective-permute-start.22) | collective-permute-done | bytes 1474592 | tf_op jit(solution)/shard_map/ppermute | solution.py:1101
  219.1 1.8 copy-done.10
  220.9 4.4 %halve.4 = (f32[4,48,1920]{2,1,0:T(8,128)S(1)}, bf16[4,48,1920]{2,1,0:T(8,128)(2,1)}) custom-call(s32[2]{0:T(128)S(1)} %copy-done.31, f32[8,48,1920]{2,1,0:T(8,128)S(1)} %copy-done.10, bf16[8,48,1920]{2,1,0:T(8,128)(2,1)} %collective-permute-done.22.part_near.part_far, f32[8,48,1920]{2,1,0:T(8,128)S(1)} %copy-done.10, ...), custom_call_target="tpu_custom_call" | custom-call | flops 1000 | bytes 1000 | tf_op jit(solution)/shard_map/halve/pallas_call | solution.py:1005
  225.3 4.8 %grad_columns.3 = (bf16[8,48,2304]{2,1,0:T(8,128)(2,1)S(1)}, bf16[8,48,2304]{2,1,0:T(8,128)(2,1)S(1)}) custom-call(s32[2]{0:T(128)S(1)} %copy-done.31, bf16[768,1024]{1,0:T(8,128)(2,1)S(1)} %copy-done.8, bf16[512,768]{1,0:T(8,128)(2,1)S(1)} %copy-done.11, bf16[768,1024]{1,0:T(8,128)(2,1)S(1)} %copy-done.8, bf16[1024,768]{1,0:T(8,128)(2,1)S(1)} %copy-done.6, ...), custom_call_target="tpu_custom_call" | custom-call | flops 1000 | bytes 1000 | tf_op jit(solution)/shard_map/grad_columns/pallas_call | solution.py:879
  230.3 1.8 collective-permute-start.27
  232.1 2.9 input_back.2.other_ref
  234.9 2.3 halve.5
  239.7 2.6 input_back.3.own_ref
  242.4 3.8 %small_sums.1 = f32[40,768]{1,0:T(8,128)S(1)} custom-call(f32[512,768]{1,0:T(8,128)S(1)} %input_back.3.own_ref, bf16[512,768]{1,0:T(8,128)(2,1)} %input_back.2.other_ref, bf16[512,768]{1,0:T(8,128)(2,1)S(1)} %bitcast.50, bf16[512,768]{1,0:T(8,128)(2,1)S(1)} %copy-done.2, f32[512,128]{1,0:T(8,128)S(1)} %copy-done.16, bf16[512,768]{1,0:T(8,128)(2,1)S(1)} %copy-done.11, ...), custom_call_target="tpu_custom_call" | custom-call | flops 1000 | bytes 1000 | tf_op jit(solution)/shard_map/small_sums/pallas_call | solution.py:970
  247.7 2.2 collective-permute-done.27.across_ref
  249.9 3.0 column_sends.2
  253.4 7.1 %collective-permute-start.29 = (bf16[48,1920]{1,0:T(8,128)(2,1)S(1)}, bf16[48,1920]{1,0:T(8,128)(2,1)S(1)}, u32[]{:S(2)}, u32[]{:S(2)}) collective-permute-start(bf16[48,1920]{1,0:T(8,128)(2,1)S(1)} %get-tuple-element.163), channel_id=1, source_target_pairs={{0,4},{1,5},{2,6},{3,7},{4,0},{5,1},{6,2},{7,3},{8,12},{9,13},{10,... | collective-permute-start | bytes 552968 | tf_op jit(solution)/shard_map/ppermute | solution.py:404
  260.5 1.8 collective-permute-start.30
  262.3 2.4 collective-permute-start.31
  264.8 3.7 %collective-permute-done.25.across_ref = bf16[4,48,2304]{2,1,0:T(8,128)(2,1)} collective-permute-done((bf16[4,48,2304]{2,1,0:T(8,128)(2,1)}, bf16[4,48,2304]{2,1,0:T(8,128)(2,1)}, u32[]{:S(2)}, u32[]{:S(2)}) %collective-permute-start.25) | collective-permute-done | bytes 884768 | tf_op jit(solution)/shard_map/ppermute | solution.py:404
  268.8 3.1 column_sends.3
  272.0 7.2 %collective-permute-start.33 = (bf16[48,2304]{1,0:T(8,128)(2,1)S(1)}, bf16[48,2304]{1,0:T(8,128)(2,1)S(1)}, u32[]{:S(2)}, u32[]{:S(2)}) collective-permute-start(bf16[48,2304]{1,0:T(8,128)(2,1)S(1)} %get-tuple-element.168), channel_id=1, source_target_pairs={{0,4},{1,5},{2,6},{3,7},{4,0},{5,1},{6,2},{7,3},{8,12},{9,13},{10,... | collective-permute-start | bytes 663560 | tf_op jit(solution)/shard_map/ppermute | solution.py:404
  279.1 2.8 state_back.1
  282.0 1.8 collective-permute-start.34
  289.2 2.5 collective-permute-done.32
  291.7 8.5 %collective-permute-done.34 = bf16[48,2304]{1,0:T(8,128)(2,1)S(1)} collective-permute-done((bf16[48,2304]{1,0:T(8,128)(2,1)S(1)}, bf16[48,2304]{1,0:T(8,128)(2,1)S(1)}, u32[]{:S(2)}, u32[]{:S(2)}) %collective-permute-start.34) | collective-permute-done | bytes 221216 | tf_op jit(solution)/shard_map/ppermute | solution.py:404
  301.8 3.9 %collective-permute-start.36 = (f32[40,768]{1,0:T(8,128)S(1)}, f32[40,768]{1,0:T(8,128)S(1)}, u32[]{:S(2)}, u32[]{:S(2)}) collective-permute-start(f32[40,768]{1,0:T(8,128)S(1)} %add.196), channel_id=1, source_target_pairs={{0,4},{1,5},{2,6},{3,7},{4,0},{5,1},{6,2},{7,3},{8,12},{9,13},{10,... | collective-permute-start | bytes 368648 | tf_op jit(solution)/shard_map/ppermute | solution.py:404
  308.7 3.7 %collective-permute-start.37 = (f32[40,768]{1,0:T(8,128)S(1)}, f32[40,768]{1,0:T(8,128)S(1)}, u32[]{:S(2)}, u32[]{:S(2)}) collective-permute-start(f32[40,768]{1,0:T(8,128)S(1)} %add.200), channel_id=1, source_target_pairs={{0,8},{1,9},{2,10},{3,11},{4,12},{5,13},{6,14},{7,15},{8,0},{9,1},... | collective-permute-start | bytes 368648 | tf_op jit(solution)/shard_map/ppermute | solution.py:404
  313.2 4.1 %collective-permute-done.37 = f32[40,768]{1,0:T(8,128)S(1)} collective-permute-done((f32[40,768]{1,0:T(8,128)S(1)}, f32[40,768]{1,0:T(8,128)S(1)}, u32[]{:S(2)}, u32[]{:S(2)}) %collective-permute-start.37) | collective-permute-done | bytes 122912 | tf_op jit(solution)/shard_map/ppermute | solution.py:404
  (264 shorter events, 69.4 us)
Async XLA Ops:
  7.2 125.2 %all-gather.2.cloned.1.call-start = ((), (), s32[]{:S(2)}) async-start(), calls=%async_computation.1 | async-start | bytes 5013504 | tf_op jit(solution)/shard_map/all_gather | solution.py:1200
  8.2 25.6 %collective-permute-start.1 = (bf16[48,1152]{1,0:T(8,128)(2,1)S(1)}, bf16[48,1152]{1,0:T(8,128)(2,1)S(1)}, u32[]{:S(2)}, u32[]{:S(2)}) collective-permute-start(bf16[48,1152]{1,0:T(8,128)(2,1)S(1)} %get-tuple-element.197), channel_id=1, source_target_pairs={{0,4},{1,5},{2,6},{3,7},{4,0},{5,1},{6,2},{7,3},{8,12},{9,13},{10,... | collective-permute-start | bytes 331784 | tf_op jit(solution)/shard_map/ppermute | solution.py:404
  11.3 22.5 %collective-permute-start.2 = (bf16[48,1152]{1,0:T(8,128)(2,1)S(1)}, bf16[48,1152]{1,0:T(8,128)(2,1)S(1)}, u32[]{:S(2)}, u32[]{:S(2)}) collective-permute-start(bf16[48,1152]{1,0:T(8,128)(2,1)S(1)} %get-tuple-element.197), channel_id=1, source_target_pairs={{0,8},{1,9},{2,10},{3,11},{4,12},{5,13},{6,14},{7,15},{8,0},{9,1},... | collective-permute-start | bytes 331784 | tf_op jit(solution)/shard_map/ppermute | solution.py:404
  13.9 20.0 %collective-permute-start.3 = (bf16[48,1152]{1,0:T(8,128)(2,1)S(1)}, bf16[48,1152]{1,0:T(8,128)(2,1)S(1)}, u32[]{:S(2)}, u32[]{:S(2)}) collective-permute-start(bf16[48,1152]{1,0:T(8,128)(2,1)S(1)} %get-tuple-element.197), channel_id=1, source_target_pairs={{0,12},{1,13},{2,14},{3,15},{4,8},{5,9},{6,10},{7,11},{8,4},{9,5},... | collective-permute-start | bytes 331784 | tf_op jit(solution)/shard_map/ppermute | solution.py:404
  13.9 47.1 %collective-permute-start = (bf16[512,768]{1,0:T(8,128)(2,1)}, bf16[512,768]{1,0:T(8,128)(2,1)S(1)}, u32[]{:S(2)}, u32[]{:S(2)}) collective-permute-start(bf16[512,768]{1,0:T(8,128)(2,1)} %bitcast.49), channel_id=1, source_target_pairs={{0,16},{16,0},{1,17},{17,1},{2,18},{18,2},{3,19},{19,3},{4,20},{20... | collective-permute-start | bytes 2359304 | tf_op jit(solution)/shard_map/ppermute | solution.py:1101
  34.8 212.9 %reduce-scatter.2.cloned.1.call-start = ((), (), s32[]{:S(2)}) async-start(), calls=%async_computation.2 | async-start | bytes 5013504 | tf_op jit(solution)/shard_map/reduce_scatter | solution.py:1235
  34.9 40.0 %copy-start.30 = (s32[2]{0:T(128)}, s32[2]{0:T(128)S(1)}, u32[]{:S(2)}) copy-start(s32[2]{0:T(128)S(1)} %pad_add_fusion.1.place) | copy-start | bytes 28
  39.1 14.0 %collective-permute-start.4 = (bf16[4,48,1152]{2,1,0:T(8,128)(2,1)S(1)}, bf16[4,48,1152]{2,1,0:T(8,128)(2,1)S(1)}, u32[]{:S(2)}, u32[]{:S(2)}) collective-permute-start(bf16[4,48,1152]{2,1,0:T(8,128)(2,1)S(1)} %copy-done.38), channel_id=1, source_target_pairs={{0,2},{1,3},{2,0},{3,1},{4,6},{5,7},{6,4},{7,5},{8,10},{9,11},{10,... | collective-permute-start | bytes 1327112 | tf_op jit(solution)/shard_map/ppermute | solution.py:404
  40.6 13.2 %collective-permute-start.7 = (bf16[48,896]{1,0:T(8,128)(2,1)S(1)}, bf16[48,896]{1,0:T(8,128)(2,1)S(1)}, u32[]{:S(2)}, u32[]{:S(2)}) collective-permute-start(bf16[48,896]{1,0:T(8,128)(2,1)S(1)} %fusion.2), channel_id=1, source_target_pairs={{0,4},{1,5},{2,6},{3,7},{4,0},{5,1},{6,2},{7,3},{8,12},{9,13},{10,... | collective-permute-start | bytes 258056 | tf_op jit(solution)/shard_map/ppermute | solution.py:404
  41.3 12.5 %collective-permute-start.8 = (bf16[48,896]{1,0:T(8,128)(2,1)S(1)}, bf16[48,896]{1,0:T(8,128)(2,1)S(1)}, u32[]{:S(2)}, u32[]{:S(2)}) collective-permute-start(bf16[48,896]{1,0:T(8,128)(2,1)S(1)} %fusion.2), channel_id=1, source_target_pairs={{0,8},{1,9},{2,10},{3,11},{4,12},{5,13},{6,14},{7,15},{8,0},{9,1},... | collective-permute-start | bytes 258056 | tf_op jit(solution)/shard_map/ppermute | solution.py:404
  44.8 9.0 %collective-permute-start.9 = (bf16[48,896]{1,0:T(8,128)(2,1)S(1)}, bf16[48,896]{1,0:T(8,128)(2,1)S(1)}, u32[]{:S(2)}, u32[]{:S(2)}) collective-permute-start(bf16[48,896]{1,0:T(8,128)(2,1)S(1)} %fusion.2), channel_id=1, source_target_pairs={{0,12},{1,13},{2,14},{3,15},{4,8},{5,9},{6,10},{7,11},{8,4},{9,5},... | collective-permute-start | bytes 258056 | tf_op jit(solution)/shard_map/ppermute | solution.py:404
  53.2 18.2 %collective-permute-start.6 = (bf16[8,48,1152]{2,1,0:T(8,128)(2,1)S(1)}, bf16[8,48,1152]{2,1,0:T(8,128)(2,1)S(1)}, u32[]{:S(2)}, u32[]{:S(2)}) collective-permute-start(bf16[8,48,1152]{2,1,0:T(8,128)(2,1)S(1)} %constant_dynamic-update-slice_fusion.refs_0_), channel_id=1, source_target_pairs={{0,16},{16,0},{1,17},{17,1},{2,18},{18,2},{3,19},{19,3},{4,20},{20... | collective-permute-start | bytes 2654216 | tf_op jit(solution)/shard_map/ppermute | solution.py:1101
  53.8 21.1 %collective-permute-start.5 = (bf16[8,48,1152]{2,1,0:T(8,128)(2,1)S(1)}, bf16[8,48,1152]{2,1,0:T(8,128)(2,1)S(1)}, u32[]{:S(2)}, u32[]{:S(2)}) collective-permute-start(bf16[8,48,1152]{2,1,0:T(8,128)(2,1)S(1)} %constant_dynamic-update-slice_fusion.refs_0_), channel_id=1, source_target_pairs={{0,1},{1,0},{2,3},{3,2},{4,5},{5,4},{6,7},{7,6},{8,9},{9,8},{10,11... | collective-permute-start | bytes 2654216 | tf_op jit(solution)/shard_map/ppermute | solution.py:404
  54.5 10.5 %collective-permute-start.10 = (bf16[4,48,896]{2,1,0:T(8,128)(2,1)S(1)}, bf16[4,48,896]{2,1,0:T(8,128)(2,1)S(1)}, u32[]{:S(2)}, u32[]{:S(2)}) collective-permute-start(bf16[4,48,896]{2,1,0:T(8,128)(2,1)S(1)} %pad_maximum_fusion.3), channel_id=1, source_target_pairs={{0,2},{1,3},{2,0},{3,1},{4,6},{5,7},{6,4},{7,5},{8,10},{9,11},{10,... | collective-permute-start | bytes 1032200 | tf_op jit(solution)/shard_map/ppermute | solution.py:404
  58.1 27.1 %collective-permute-start.12 = (bf16[48,2048]{1,0:T(8,128)(2,1)}, bf16[48,2048]{1,0:T(8,128)(2,1)S(1)}, u32[]{:S(2)}, u32[]{:S(2)}) collective-permute-start(bf16[48,2048]{1,0:T(8,128)(2,1)} %slice.152), channel_id=1, source_target_pairs={{0,4},{1,5},{2,6},{3,7},{4,0},{5,1},{6,2},{7,3},{8,12},{9,13},{10,... | collective-permute-start | bytes 589832 | tf_op jit(solution)/shard_map/ppermute | solution.py:404
  61.1 25.9 %collective-permute-start.13 = (bf16[48,2048]{1,0:T(8,128)(2,1)}, bf16[48,2048]{1,0:T(8,128)(2,1)S(1)}, u32[]{:S(2)}, u32[]{:S(2)}) collective-permute-start(bf16[48,2048]{1,0:T(8,128)(2,1)} %slice.152), channel_id=1, source_target_pairs={{0,8},{1,9},{2,10},{3,11},{4,12},{5,13},{6,14},{7,15},{8,0},{9,1},... | collective-permute-start | bytes 589832 | tf_op jit(solution)/shard_map/ppermute | solution.py:404
  65.0 21.9 %collective-permute-start.14 = (bf16[48,2048]{1,0:T(8,128)(2,1)}, bf16[48,2048]{1,0:T(8,128)(2,1)S(1)}, u32[]{:S(2)}, u32[]{:S(2)}) collective-permute-start(bf16[48,2048]{1,0:T(8,128)(2,1)} %slice.152), channel_id=1, source_target_pairs={{0,12},{1,13},{2,14},{3,15},{4,8},{5,9},{6,10},{7,11},{8,4},{9,5},... | collective-permute-start | bytes 589832 | tf_op jit(solution)/shard_map/ppermute | solution.py:404
  71.4 3.5 %collective-permute-start.11 = (bf16[8,48,1152]{2,1,0:T(8,128)(2,1)S(1)}, bf16[8,48,1152]{2,1,0:T(8,128)(2,1)S(1)}, u32[]{:S(2)}, u32[]{:S(2)}) collective-permute-start(bf16[8,48,1152]{2,1,0:T(8,128)(2,1)S(1)} %collective-permute-done.6.refs_2_), channel_id=1, source_target_pairs={{0,1},{1,0},{2,3},{3,2},{4,5},{5,4},{6,7},{7,6},{8,9},{9,8},{10,11... | collective-permute-start | bytes 2654216 | tf_op jit(solution)/shard_map/ppermute | solution.py:404
  88.8 19.4 %collective-permute-start.19 = (bf16[4,48,2048]{2,1,0:T(8,128)(2,1)}, bf16[4,48,2048]{2,1,0:T(8,128)(2,1)}, u32[]{:S(2)}, u32[]{:S(2)}) collective-permute-start(bf16[4,48,2048]{2,1,0:T(8,128)(2,1)} %pad_maximum_fusion.1.refs_4_), channel_id=1, source_target_pairs={{0,2},{1,3},{2,0},{3,1},{4,6},{5,7},{6,4},{7,5},{8,10},{9,11},{10,... | collective-permute-start | bytes 2359304 | tf_op jit(solution)/shard_map/ppermute | solution.py:404
  89.7 19.0 %collective-permute-start.16 = (bf16[8,48,896]{2,1,0:T(8,128)(2,1)}, bf16[8,48,896]{2,1,0:T(8,128)(2,1)}, u32[]{:S(2)}, u32[]{:S(2)}) collective-permute-start(bf16[8,48,896]{2,1,0:T(8,128)(2,1)} %constant_dynamic-update-slice_fusion.5.refs_0_), channel_id=1, source_target_pairs={{0,16},{16,0},{1,17},{17,1},{2,18},{18,2},{3,19},{19,3},{4,20},{20... | collective-permute-start | bytes 2064392 | tf_op jit(solution)/shard_map/ppermute | solution.py:1101
  90.0 22.8 %collective-permute-start.18 = (bf16[4,48,2048]{2,1,0:T(8,128)(2,1)}, bf16[4,48,2048]{2,1,0:T(8,128)(2,1)}, u32[]{:S(2)}, u32[]{:S(2)}) collective-permute-start(bf16[4,48,2048]{2,1,0:T(8,128)(2,1)} %pad_maximum_fusion.1.refs_4_), channel_id=1, source_target_pairs={{0,1},{1,0},{2,3},{3,2},{4,5},{5,4},{6,7},{7,6},{8,9},{9,8},{10,11... | collective-permute-start | bytes 2359304 | tf_op jit(solution)/shard_map/ppermute | solution.py:404
  108.2 4.6 %collective-permute-start.20 = (bf16[4,48,2048]{2,1,0:T(8,128)(2,1)}, bf16[4,48,2048]{2,1,0:T(8,128)(2,1)}, u32[]{:S(2)}, u32[]{:S(2)}) collective-permute-start(bf16[4,48,2048]{2,1,0:T(8,128)(2,1)} %collective-permute-done.19.refs_6_), channel_id=1, source_target_pairs={{0,1},{1,0},{2,3},{3,2},{4,5},{5,4},{6,7},{7,6},{8,9},{9,8},{10,11... | collective-permute-start | bytes 2359304 | tf_op jit(solution)/shard_map/ppermute | solution.py:404
  108.2 3.6 %collective-permute-start.15 = (bf16[8,48,896]{2,1,0:T(8,128)(2,1)}, bf16[8,48,896]{2,1,0:T(8,128)(2,1)}, u32[]{:S(2)}, u32[]{:S(2)}) collective-permute-start(bf16[8,48,896]{2,1,0:T(8,128)(2,1)} %constant_dynamic-update-slice_fusion.5.refs_0_), channel_id=1, source_target_pairs={{0,1},{1,0},{2,3},{3,2},{4,5},{5,4},{6,7},{7,6},{8,9},{9,8},{10,11... | collective-permute-start | bytes 2064392 | tf_op jit(solution)/shard_map/ppermute | solution.py:404
  108.7 4.1 %collective-permute-start.17 = (bf16[8,48,896]{2,1,0:T(8,128)(2,1)}, bf16[8,48,896]{2,1,0:T(8,128)(2,1)}, u32[]{:S(2)}, u32[]{:S(2)}) collective-permute-start(bf16[8,48,896]{2,1,0:T(8,128)(2,1)} %collective-permute-done.16.refs_2_), channel_id=1, source_target_pairs={{0,1},{1,0},{2,3},{3,2},{4,5},{5,4},{6,7},{7,6},{8,9},{9,8},{10,11... | collective-permute-start | bytes 2064392 | tf_op jit(solution)/shard_map/ppermute | solution.py:404
  174.4 5.4 %collective-permute-start.21 = (bf16[8,48,3840]{2,1,0:T(8,128)(2,1)S(1)}, bf16[8,48,3840]{2,1,0:T(8,128)(2,1)S(1)}, u32[]{:S(2)}, u32[]{:S(2)}) collective-permute-start(bf16[8,48,3840]{2,1,0:T(8,128)(2,1)S(1)} %get-tuple-element.137), channel_id=1, source_target_pairs={{0,1},{1,0},{2,3},{3,2},{4,5},{5,4},{6,7},{7,6},{8,9},{9,8},{10,11... | collective-permute-start | bytes 8847368 | tf_op jit(solution)/shard_map/ppermute | solution.py:404
  184.4 34.6 %collective-permute-start.22 = (bf16[8,48,1920]{2,1,0:T(8,128)(2,1)}, bf16[8,48,1920]{2,1,0:T(8,128)(2,1)}, u32[]{:S(2)}, u32[]{:S(2)}) collective-permute-start(bf16[8,48,1920]{2,1,0:T(8,128)(2,1)} %get-tuple-element.138), channel_id=1, source_target_pairs={{0,16},{16,0},{1,17},{17,1},{2,18},{18,2},{3,19},{19,3},{4,20},{20... | collective-permute-start | bytes 4423688 | tf_op jit(solution)/shard_map/ppermute | solution.py:1101
  230.2 4.7 %collective-permute-start.23 = (bf16[8,48,2304]{2,1,0:T(8,128)(2,1)S(1)}, bf16[8,48,2304]{2,1,0:T(8,128)(2,1)S(1)}, u32[]{:S(2)}, u32[]{:S(2)}) collective-permute-start(bf16[8,48,2304]{2,1,0:T(8,128)(2,1)S(1)} %get-tuple-element.149), channel_id=1, source_target_pairs={{0,1},{1,0},{2,3},{3,2},{4,5},{5,4},{6,7},{7,6},{8,9},{9,8},{10,11... | collective-permute-start | bytes 5308424 | tf_op jit(solution)/shard_map/ppermute | solution.py:404
  230.3 19.7 %collective-permute-start.27 = (bf16[4,48,1920]{2,1,0:T(8,128)(2,1)}, bf16[4,48,1920]{2,1,0:T(8,128)(2,1)}, u32[]{:S(2)}, u32[]{:S(2)}) collective-permute-start(bf16[4,48,1920]{2,1,0:T(8,128)(2,1)} %get-tuple-element.146), channel_id=1, source_target_pairs={{0,2},{1,3},{2,0},{3,1},{4,6},{5,7},{6,4},{7,5},{8,10},{9,11},{10,... | collective-permute-start | bytes 2211848 | tf_op jit(solution)/shard_map/ppermute | solution.py:404
  238.4 30.0 %collective-permute-start.25 = (bf16[4,48,2304]{2,1,0:T(8,128)(2,1)}, bf16[4,48,2304]{2,1,0:T(8,128)(2,1)}, u32[]{:S(2)}, u32[]{:S(2)}) collective-permute-start(bf16[4,48,2304]{2,1,0:T(8,128)(2,1)} %get-tuple-element.153), channel_id=1, source_target_pairs={{0,2},{1,3},{2,0},{3,1},{4,6},{5,7},{6,4},{7,5},{8,10},{9,11},{10,... | collective-permute-start | bytes 2654216 | tf_op jit(solution)/shard_map/ppermute | solution.py:404
  239.2 32.7 %collective-permute-start.24 = (bf16[512,768]{1,0:T(8,128)(2,1)}, bf16[512,768]{1,0:T(8,128)(2,1)}, u32[]{:S(2)}, u32[]{:S(2)}) collective-permute-start(bf16[512,768]{1,0:T(8,128)(2,1)} %input_back.2.other_ref), channel_id=1, source_target_pairs={{0,16},{16,0},{1,17},{17,1},{2,18},{18,2},{3,19},{19,3},{4,20},{20... | collective-permute-start | bytes 2359304 | tf_op jit(solution)/shard_map/ppermute | solution.py:1101
  246.2 22.6 %copy-start.19 = (f32[4,48,2304]{2,1,0:T(8,128)S(1)}, f32[4,48,2304]{2,1,0:T(8,128)}, u32[]{:S(2)}) copy-start(f32[4,48,2304]{2,1,0:T(8,128)} %copy-done.18) | copy-start | bytes 5308420
  246.2 1.4 collective-permute-start.26
  252.9 26.2 %copy-start.5 = (f32[512,768]{1,0:T(8,128)S(1)}, f32[512,768]{1,0:T(8,128)}, u32[]{:S(2)}) copy-start(f32[512,768]{1,0:T(8,128)} %copy-done.4) | copy-start | bytes 4718596
  252.9 26.2 %copy-start.17 = (f32[512,128]{1,0:T(8,128)S(1)}, f32[512,128]{1,0:T(8,128)}, u32[]{:S(2)}) copy-start(f32[512,128]{1,0:T(8,128)} %pad_convert_fusion.mask_ref) | copy-start | bytes 786436
  252.9 26.2 %copy-start.28 = (f32[8,768]{1,0:T(8,128)S(1)}, f32[8,768]{1,0:T(8,128)}, u32[]{:S(2)}) copy-start(f32[8,768]{1,0:T(8,128)} %pad.39.tap_ref) | copy-start | bytes 73732
  252.9 9.4 %collective-permute-start.28 = (f32[40,768]{1,0:T(8,128)S(1)}, f32[40,768]{1,0:T(8,128)S(1)}, u32[]{:S(2)}, u32[]{:S(2)}) collective-permute-start(f32[40,768]{1,0:T(8,128)S(1)} %add.191), channel_id=1, source_target_pairs={{0,16},{16,0},{1,17},{17,1},{2,18},{18,2},{3,19},{19,3},{4,20},{20... | collective-permute-start | bytes 368648 | tf_op jit(solution)/shard_map/ppermute | solution.py:1101
  253.4 28.6 %collective-permute-start.29 = (bf16[48,1920]{1,0:T(8,128)(2,1)S(1)}, bf16[48,1920]{1,0:T(8,128)(2,1)S(1)}, u32[]{:S(2)}, u32[]{:S(2)}) collective-permute-start(bf16[48,1920]{1,0:T(8,128)(2,1)S(1)} %get-tuple-element.163), channel_id=1, source_target_pairs={{0,4},{1,5},{2,6},{3,7},{4,0},{5,1},{6,2},{7,3},{8,12},{9,13},{10,... | collective-permute-start | bytes 552968 | tf_op jit(solution)/shard_map/ppermute | solution.py:404
  260.5 23.3 %collective-permute-start.30 = (bf16[48,1920]{1,0:T(8,128)(2,1)S(1)}, bf16[48,1920]{1,0:T(8,128)(2,1)S(1)}, u32[]{:S(2)}, u32[]{:S(2)}) collective-permute-start(bf16[48,1920]{1,0:T(8,128)(2,1)S(1)} %get-tuple-element.164), channel_id=1, source_target_pairs={{0,8},{1,9},{2,10},{3,11},{4,12},{5,13},{6,14},{7,15},{8,0},{9,1},... | collective-permute-start | bytes 552968 | tf_op jit(solution)/shard_map/ppermute | solution.py:404
  262.3 23.0 %collective-permute-start.31 = (bf16[48,1920]{1,0:T(8,128)(2,1)S(1)}, bf16[48,1920]{1,0:T(8,128)(2,1)S(1)}, u32[]{:S(2)}, u32[]{:S(2)}) collective-permute-start(bf16[48,1920]{1,0:T(8,128)(2,1)S(1)} %get-tuple-element.165), channel_id=1, source_target_pairs={{0,12},{1,13},{2,14},{3,15},{4,8},{5,9},{6,10},{7,11},{8,4},{9,5},... | collective-permute-start | bytes 552968 | tf_op jit(solution)/shard_map/ppermute | solution.py:404
  268.4 18.4 %collective-permute-start.40 = (bf16[192,768]{1,0:T(8,128)(2,1)S(1)}, bf16[192,768]{1,0:T(8,128)(2,1)S(1)}, u32[]{:S(2)}, u32[]{:S(2)}) collective-permute-start(bf16[192,768]{1,0:T(8,128)(2,1)S(1)} %copy-done.43), channel_id=1, source_target_pairs={{0,16},{16,0},{1,17},{17,1},{2,18},{18,2},{3,19},{19,3},{4,20},{20... | collective-permute-start | bytes 884744 | tf_op jit(solution)/shard_map/ppermute | solution.py:1101
  272.0 19.8 %collective-permute-start.33 = (bf16[48,2304]{1,0:T(8,128)(2,1)S(1)}, bf16[48,2304]{1,0:T(8,128)(2,1)S(1)}, u32[]{:S(2)}, u32[]{:S(2)}) collective-permute-start(bf16[48,2304]{1,0:T(8,128)(2,1)S(1)} %get-tuple-element.168), channel_id=1, source_target_pairs={{0,4},{1,5},{2,6},{3,7},{4,0},{5,1},{6,2},{7,3},{8,12},{9,13},{10,... | collective-permute-start | bytes 663560 | tf_op jit(solution)/shard_map/ppermute | solution.py:404
  282.0 18.2 %collective-permute-start.34 = (bf16[48,2304]{1,0:T(8,128)(2,1)S(1)}, bf16[48,2304]{1,0:T(8,128)(2,1)S(1)}, u32[]{:S(2)}, u32[]{:S(2)}) collective-permute-start(bf16[48,2304]{1,0:T(8,128)(2,1)S(1)} %get-tuple-element.169), channel_id=1, source_target_pairs={{0,8},{1,9},{2,10},{3,11},{4,12},{5,13},{6,14},{7,15},{8,0},{9,1},... | collective-permute-start | bytes 663560 | tf_op jit(solution)/shard_map/ppermute | solution.py:404
  283.8 16.4 %collective-permute-start.35 = (bf16[48,2304]{1,0:T(8,128)(2,1)S(1)}, bf16[48,2304]{1,0:T(8,128)(2,1)S(1)}, u32[]{:S(2)}, u32[]{:S(2)}) collective-permute-start(bf16[48,2304]{1,0:T(8,128)(2,1)S(1)} %get-tuple-element.170), channel_id=1, source_target_pairs={{0,12},{1,13},{2,14},{3,15},{4,8},{5,9},{6,10},{7,11},{8,4},{9,5},... | collective-permute-start | bytes 663560 | tf_op jit(solution)/shard_map/ppermute | solution.py:404
  285.4 20.3 %collective-permute-start.39 = (bf16[48,1920]{1,0:T(8,128)(2,1)S(1)}, bf16[48,1920]{1,0:T(8,128)(2,1)S(1)}, u32[]{:S(2)}, u32[]{:S(2)}) collective-permute-start(bf16[48,1920]{1,0:T(8,128)(2,1)S(1)} %add_convert_fusion.4), channel_id=1, source_target_pairs={{0,16},{16,0},{1,17},{17,1},{2,18},{18,2},{3,19},{19,3},{4,20},{20... | collective-permute-start | bytes 552968 | tf_op jit(solution)/shard_map/ppermute | solution.py:1101
  286.8 4.9 %collective-permute-start.32 = (f32[40,768]{1,0:T(8,128)S(1)}, f32[40,768]{1,0:T(8,128)S(1)}, u32[]{:S(2)}, u32[]{:S(2)}) collective-permute-start(f32[40,768]{1,0:T(8,128)S(1)} %add.192), channel_id=1, source_target_pairs={{0,2},{1,3},{2,0},{3,1},{4,6},{5,7},{6,4},{7,5},{8,10},{9,11},{10,... | collective-permute-start | bytes 368648 | tf_op jit(solution)/shard_map/ppermute | solution.py:404
  300.3 12.0 %collective-permute-start.38 = (bf16[48,2304]{1,0:T(8,128)(2,1)S(1)}, bf16[48,2304]{1,0:T(8,128)(2,1)S(1)}, u32[]{:S(2)}, u32[]{:S(2)}) collective-permute-start(bf16[48,2304]{1,0:T(8,128)(2,1)S(1)} %add_convert_fusion.3), channel_id=1, source_target_pairs={{0,16},{16,0},{1,17},{17,1},{2,18},{18,2},{3,19},{19,3},{4,20},{20... | collective-permute-start | bytes 663560 | tf_op jit(solution)/shard_map/ppermute | solution.py:1101
  301.8 6.8 %collective-permute-start.36 = (f32[40,768]{1,0:T(8,128)S(1)}, f32[40,768]{1,0:T(8,128)S(1)}, u32[]{:S(2)}, u32[]{:S(2)}) collective-permute-start(f32[40,768]{1,0:T(8,128)S(1)} %add.196), channel_id=1, source_target_pairs={{0,4},{1,5},{2,6},{3,7},{4,0},{5,1},{6,2},{7,3},{8,12},{9,13},{10,... | collective-permute-start | bytes 368648 | tf_op jit(solution)/shard_map/ppermute | solution.py:404
  308.7 8.7 %collective-permute-start.37 = (f32[40,768]{1,0:T(8,128)S(1)}, f32[40,768]{1,0:T(8,128)S(1)}, u32[]{:S(2)}, u32[]{:S(2)}) collective-permute-start(f32[40,768]{1,0:T(8,128)S(1)} %add.200), channel_id=1, source_target_pairs={{0,8},{1,9},{2,10},{3,11},{4,12},{5,13},{6,14},{7,15},{8,0},{9,1},... | collective-permute-start | bytes 368648 | tf_op jit(solution)/shard_map/ppermute | solution.py:404
  (48 other events, 264.5 us)
Sparse Core Ops, SparseCore 0:
  34.9 65.9 all-gather.1
  149.1 82.6 reduce-scatter.1
where the time goes:
time: 334 us; the launch traced here: 328 us
  Pallas kernels  132 us (40%)
  starting transfers between devices  64.6 us (19%)
  waiting for transfers between devices  61.2 us (18%)
  local copies, waits for them, and re-layouts  38.6 us (12%)
  other arithmetic  17 us (5%)
  between operations  15.2 us (5%)
    ppermute x32, starting transfers between devices, exchange(): return lax.ppermute(values, 'page', [(i, i ^ mask) for i in range(count)])  57.4 us
    ppermute x32, waiting for transfers between devices, exchange(): return lax.ppermute(values, 'page', [(i, i ^ mask) for i in range(count)])  49.5 us
    pallas_call x1, Pallas kernels, attend_back(): pl.pallas_call(attend_back_kernel, grid_spec=pltpu.PrefetchScalarGridSpec...  24.6 us
    unnamed x119, local copies, waits for them, and re-layouts  21.3 us
    pallas_call x1, Pallas kernels, up_forward(): pl.pallas_call(functools.partial(up_kernel, groups), grid_spec=pltpu.Pref...  19.6 us
    pallas_call x1, Pallas kernels, ffn_back(): pl.pallas_call(ffn_back_kernel, grid=(hidden_width // tile,), in_specs=[t...  14.5 us
    pallas_call x1, Pallas kernels, attend(): pl.pallas_call(attend_kernel, grid_spec=pltpu.PrefetchScalarGridSpec(num_...  12.9 us
    ppermute x9, waiting for transfers between devices, swap(): return lax.ppermute(values, 'mod', [(0, 1), (1, 0)])  11.7 us
  transfers between devices with their start and end apart: 43, of which 16 were waited for; matrix products, arithmetic and copies ran while one was open for 10% of the time, Pallas kernels for 35%

commit v1 on v0

--- a/solution.py
+++ b/solution.py
@@ -1138,6 +1138,15 @@
     pack_qkv = jnp.concatenate([w_query, w_key, w_value], axis=1)
     pack_rest = jnp.concatenate([w_out, w_up], axis=1)
     other_low = swap(own_low)
+    if fast:
+        column_qkv = column_of(half_columns(pack_qkv, is_text))
+        table_pos, table_x, table_y, b_out, b_down, b_query, b_value, b_up = after(
+            (table_pos, table_x, table_y, b_out, b_down, b_query, b_value, b_up), column_qkv
+        )
+        gain_one, bias_one, gain_two, bias_two, conv_weight = after(
+            (gain_one, bias_one, gain_two, bias_two, conv_weight), column_qkv
+        )
+        segments, box_x, box_y = after((segments, box_x, box_y), column_qkv)
     page_ids, pos_bins, bins_x, bins_y = token_ids(segments[0], box_x[0], box_y[0])
     bounds = page_bounds(segments[0], is_text)
     own_pages = jnp.where(is_text, page_ids[0], page_ids[1])
@@ -1183,7 +1192,6 @@
     bias_up = b_up[None]
     if fast:
         split = (pack_rest.shape[1] // 2 + 127) // 256 * 256
-        column_qkv = column_of(half_columns(pack_qkv, is_text))
         early = (features, own_feats, own_flip, tables, bounds, masks, vectors, biases, taps)
         parts_near = column_parts(after(half_columns(pack_rest[:, :split], is_text), column_qkv))
         w_down = after(w_down, column_qkv)
@@ -1307,11 +1315,11 @@
         arrived_rest = [after(part, grad_in) for part in arrived_rest]
         total_rest = column_total(own_rest, arrived_rest)
         far_rest = swap(total_rest)
-        packed = both_sum(after(packed, total_rest), 2)
+        packed = both_sum(both_sum(after(packed, total_rest), 2), 4)
         arrived_qkv = [after(part, packed) for part in arrived_qkv]
         total_qkv = column_total(own_qkv, arrived_qkv)
         far_qkv = swap(total_qkv)
-        packed = both_sum(both_sum(after(packed, total_qkv), 4), 8)
+        packed = both_sum(after(packed, total_qkv), 8)
     g_tables = packed[28:34].reshape(HEADS, 3, LANES)
     if fast:
         shard_rest = jnp.where(

time: 334 us -> 313 us (0.937)
  waiting for transfers between devices: 61.2 us -> 54.6 us
  starting transfers between devices: 64.6 us -> 58.3 us
  local copies, waits for them, and re-layouts: 38.6 us -> 33.1 us
    ppermute x32, starting transfers between devices: 57.4 us -> 46.7 us  [exchange(): return lax.ppermute(values, 'page', [(i, i ^ mask) for i in range(count)])]
    ppermute x32, waiting for transfers between devices: 49.5 us -> 42.4 us  [exchange(): return lax.ppermute(values, 'page', [(i, i ^ mask) for i in range(count)])]
    ppermute x9, starting transfers between devices: 7.13 us -> 11.5 us  [swap(): return lax.ppermute(values, 'mod', [(0, 1), (1, 0)])]
    another operation x8, local copies, waits for them, and re-layouts: 4.78 us -> 0.68 us  [local(): jnp.stack([b_out, gain_one, bias_one, b_down, gain_two, bias_two, jnp.zer...]
    unnamed x119 -> x137, local copies, waits for them, and re-layouts: 21.3 us -> 22.5 us
  transfers between devices with their start and end apart: 43 -> 43, of which waited for: 16 -> 16; matrix products, arithmetic and copies ran while one was open for 10% -> 10% of each run, Pallas kernels for 35% -> 37%
where the time goes in v1:
time: 313 us; the launch traced here: 308 us
  Pallas kernels  131 us (42%)
  starting transfers between devices  58.3 us (19%)
  waiting for transfers between devices  54.6 us (17%)
  local copies, waits for them, and re-layouts  33.1 us (11%)
  between operations  15.5 us (5%)
  other arithmetic  15.1 us (5%)
    ppermute x32, starting transfers between devices, exchange(): return lax.ppermute(values, 'page', [(i, i ^ mask) for i in range(count)])  46.7 us
    ppermute x32, waiting for transfers between devices, exchange(): return lax.ppermute(values, 'page', [(i, i ^ mask) for i in range(count)])  42.4 us
    pallas_call x1, Pallas kernels, attend_back(): pl.pallas_call(attend_back_kernel, grid_spec=pltpu.PrefetchScalarGridSpec...  24.4 us
    unnamed x137, local copies, waits for them, and re-layouts  22.5 us
    pallas_call x1, Pallas kernels, up_forward(): pl.pallas_call(functools.partial(up_kernel, groups), grid_spec=pltpu.Pref...  19.6 us
    pallas_call x1, Pallas kernels, ffn_back(): pl.pallas_call(ffn_back_kernel, grid=(hidden_width // tile,), in_specs=[t...  14.5 us
    pallas_call x1, Pallas kernels, attend(): pl.pallas_call(attend_kernel, grid_spec=pltpu.PrefetchScalarGridSpec(num_...  12.8 us
    ppermute x9, waiting for transfers between devices, swap(): return lax.ppermute(values, 'mod', [(0, 1), (1, 0)])  12.1 us
  transfers between devices with their start and end apart: 43, of which 16 were waited for; matrix products, arithmetic and copies ran while one was open for 10% of the time, Pallas kernels for 37%

profile of v1, /device:TPU:0, one launch (start us, length us, event | category | flops | bytes accessed | tf_op | source)
XLA Modules:
  0.0 308.0 jit_solution(14919888042519552937)
XLA Ops:
  8.3 3.1 %collective-permute-start = (bf16[48,1152]{1,0:T(8,128)(2,1)S(1)}, bf16[48,1152]{1,0:T(8,128)(2,1)S(1)}, u32[]{:S(2)}, u32[]{:S(2)}) collective-permute-start(bf16[48,1152]{1,0:T(8,128)(2,1)S(1)} %get-tuple-element.229), channel_id=1, source_target_pairs={{0,4},{1,5},{2,6},{3,7},{4,0},{5,1},{6,2},{7,3},{8,12},{9,13},{10,... | collective-permute-start | bytes 331784 | tf_op jit(solution)/shard_map/ppermute | solution.py:404
  11.4 2.6 collective-permute-start.1
  14.0 1.7 collective-permute-start.3
  18.2 1.9 fusion.13
  20.3 2.4 collective-permute-done.1
  22.8 1.6 collective-permute-start.4
  24.4 1.7 collective-permute-start.7
  46.2 2.2 collective-permute-start.13
  48.7 2.9 collective-permute-done.10
  51.6 2.5 collective-permute-start.14
  54.8 2.5 collective-permute-done.6.refs_2_
  57.4 2.1 broadcast_select_fusion.1
  62.0 5.5 %project.1 = (bf16[512,768]{1,0:T(8,128)(2,1)S(1)}, bf16[1024,1536]{1,0:T(8,128)(2,1)S(1)}, bf16[768,2304]{1,0:T(8,128)(2,1)S(1)}, bf16[768,1024]{1,0:T(8,128)(2,1)S(1)}) custom-call(s32[2]{0:T(128)S(1)} %pad_add_fusion.1.place, bf16[1024,768]{1,0:T(8,128)(2,1)S(1)} %pad_maximum_fusion.mixed_ref, f32[1,2304]{1,0:T(1,128)S(1)} %broadcast_in_dim.67.bias_ref, ...), custom_call_target="tpu_custom_call" | custom-call | flops 1000 | bytes 1000 | tf_op jit(solution)/shard_map/project/pallas_call | solution.py:438
  67.5 1.6 copy-done
  71.2 1.9 pad_maximum_fusion.1.refs_4_
  75.0 12.8 %attend.1.context_ref = bf16[512,768]{1,0:T(8,128)(2,1)} custom-call(s32[32]{0:T(128)} %pad_add_fusion.2.bounds, bf16[512,768]{1,0:T(8,128)(2,1)} %copy-done.14, bf16[1024,1536]{1,0:T(8,128)(2,1)} %copy-done, bf16[1024,1536]{1,0:T(8,128)(2,1)} %copy-done, bf16[1024,128]{1,0:T(8,128)(2,1)} %copy-done.38, bf16[512,128]{1,0:T(8,128)(2,1)} %slice_select_fusion.1.own_feat_ref, ...), custom_call_target="tpu_custom_call" | custom-call | flops 1000 | bytes 1000 | tf_op jit(solution)/shard_map/attend/pallas_call | solution.py:329
  87.9 5.5 %collective-permute-done.19.refs_6_ = bf16[4,48,2048]{2,1,0:T(8,128)(2,1)} collective-permute-done((bf16[4,48,2048]{2,1,0:T(8,128)(2,1)}, bf16[4,48,2048]{2,1,0:T(8,128)(2,1)}, u32[]{:S(2)}, u32[]{:S(2)}) %collective-permute-start.19) | collective-permute-done | bytes 786464 | tf_op jit(solution)/shard_map/ppermute | solution.py:404
  93.9 3.1 %collective-permute-done.15.refs_1_ = bf16[8,48,896]{2,1,0:T(8,128)(2,1)} collective-permute-done((bf16[8,48,896]{2,1,0:T(8,128)(2,1)}, bf16[8,48,896]{2,1,0:T(8,128)(2,1)}, u32[]{:S(2)}, u32[]{:S(2)}) %collective-permute-start.15) | collective-permute-done | bytes 688160 | tf_op jit(solution)/shard_map/ppermute | solution.py:404
  97.9 19.6 %up_forward.1 = (f32[512,768]{1,0:T(8,128)}, f32[512,128]{1,0:T(8,128)}, bf16[512,768]{1,0:T(8,128)(2,1)}, bf16[768,512]{1,0:T(8,128)(2,1)}, bf16[768,512]{1,0:T...) custom-call(s32[2]{0:T(128)} %copy-done.30, ...), custom_call_target="tpu_custom_call" | custom-call | flops 1000 | bytes 1000 | tf_op jit(solution)/shard_map/up_forward/pallas_call | solution.py:615
  117.6 10.1 %down_forward.1 = (bf16[512,768]{1,0:T(8,128)(2,1)}, f32[512,768]{1,0:T(8,128)}, bf16[512,768]{1,0:T(8,128)(2,1)}, f32[8,768]{1,0:T(8,128)}) custom-call(bf16[512,3072]{1,0:T(8,128)(2,1)} %get-tuple-element.151.active_ref, bf16[3072,768]{1,0:T(8,128)(2,1)} %all-gather.2.cloned.1.call-done.weight_ref.refs_6_, f32[512,768]{1,0:T(8,128)} %get-tuple-element.153.unit_ref.refs_3_, ...), custom_call_target="tpu_custom_call" | custom-call | flops 1000 | bytes 1000 | tf_op jit(solution)/shard_map/down_forward/pallas_call | solution.py:701
  127.7 6.4 %grad_rows.1 = bf16[3072,768]{1,0:T(8,128)(2,1)} custom-call(bf16[3072,512]{1,0:T(8,128)(2,1)} %get-tuple-element.156.x_ref, bf16[512,768]{1,0:T(8,128)(2,1)} %get-tuple-element.157.h_ref.refs_0_), custom_call_target="tpu_custom_call" | custom-call | flops 1000 | bytes 1000 | tf_op jit(solution)/shard_map/grad_rows/pallas_call | solution.py:813
  134.1 14.5 %ffn_back.1 = (bf16[512,3072]{1,0:T(8,128)(2,1)}, f32[1,3072]{1,0:T(1,128)}, f32[512,768]{1,0:T(8,128)}, bf16[512,768]{1,0:T(8,128)(2,1)}, bf16[512,768]{1,0:T(8,128)(2,1)}, /*index=5*/f32[8,768]{1,0:T(8,128)}) custom-call(bf16[512,768]{1,0:T(8,128)(2,1)} %get-tuple-element.157.h_ref.refs_0_, bf16[512,3072]{1,0:T(8,128)(2,1)} %get-tuple-element.158.refs_1_, ...), custom_call_target="tpu_custom_call" | custom-call | flops 1000 | bytes 1000 | tf_op jit(solution)/shard_map/ffn_back/pallas_call | solution.py:770
  148.6 2.1 copy-done.15
  154.2 5.4 %grad_columns.2 = (bf16[8,48,3840]{2,1,0:T(8,128)(2,1)S(1)}, bf16[8,48,3840]{2,1,0:T(8,128)(2,1)S(1)}) custom-call(s32[2]{0:T(128)S(1)} %copy-done.31, bf16[768,512]{1,0:T(8,128)(2,1)S(1)} %copy-done.26, bf16[512,768]{1,0:T(8,128)(2,1)S(1)} %copy-done.27, bf16[768,512]{1,0:T(8,128)(2,1)S(1)} %copy-done.25, bf16[512,3072]{1,0:T(8,128)(2,1)S(1)} %copy-done.15), custom_call_target="tpu_custom_call" | custom-call | flops 1000 | bytes 1000 | tf_op jit(solution)/shard_map/grad_columns/pallas_call | solution.py:879
  159.7 5.3 %collective-permute-done.21.part_near.part_far = bf16[8,48,3840]{2,1,0:T(8,128)(2,1)S(1)} collective-permute-done((bf16[8,48,3840]{2,1,0:T(8,128)(2,1)S(1)}, bf16[8,48,3840]{2,1,0:T(8,128)(2,1)S(1)}, u32[]{:S(2)}, u32[]{:S(2)}) %collective-permute-start.21) | collective-permute-done | bytes 2949152 | tf_op jit(solution)/shard_map/ppermute | solution.py:404
  165.0 3.0 halve.3
  168.0 1.6 copy-done.9
  171.1 24.4 %attend_back.1 = (bf16[512,768]{1,0:T(8,128)(2,1)}, bf16[1024,768]{1,0:T(8,128)(2,1)}, bf16[1024,768]{1,0:T(8,128)(2,1)}, f32[12,8,128]{2,1,0:T(8,128)}) custom-call(s32[32]{0:T(128)} %pad_add_fusion.2.bounds, bf16[512,768]{1,0:T(8,128)(2,1)} %copy-done.14, bf16[1024,1536]{1,0:T(8,128)(2,1)} %copy-done, bf16[1024,1536]{1,0:T(8,128)(2,1)} %copy-done, ...), custom_call_target="tpu_custom_call" | custom-call | flops 1000 | bytes 1000 | tf_op jit(solution)/shard_map/attend_back/pallas_call | solution.py:355
  195.5 8.7 %collective-permute-done.22.part_near.part_far = bf16[8,48,1920]{2,1,0:T(8,128)(2,1)} collective-permute-done((bf16[8,48,1920]{2,1,0:T(8,128)(2,1)}, bf16[8,48,1920]{2,1,0:T(8,128)(2,1)}, u32[]{:S(2)}, u32[]{:S(2)}) %collective-permute-start.22) | collective-permute-done | bytes 1474592 | tf_op jit(solution)/shard_map/ppermute | solution.py:1101
  204.2 1.8 copy-done.10
  206.1 4.4 %halve.4 = (f32[4,48,1920]{2,1,0:T(8,128)S(1)}, bf16[4,48,1920]{2,1,0:T(8,128)(2,1)}) custom-call(s32[2]{0:T(128)S(1)} %copy-done.31, f32[8,48,1920]{2,1,0:T(8,128)S(1)} %copy-done.10, bf16[8,48,1920]{2,1,0:T(8,128)(2,1)} %collective-permute-done.22.part_near.part_far, f32[8,48,1920]{2,1,0:T(8,128)S(1)} %copy-done.10, ...), custom_call_target="tpu_custom_call" | custom-call | flops 1000 | bytes 1000 | tf_op jit(solution)/shard_map/halve/pallas_call | solution.py:1005
  210.5 4.8 %grad_columns.3 = (bf16[8,48,2304]{2,1,0:T(8,128)(2,1)S(1)}, bf16[8,48,2304]{2,1,0:T(8,128)(2,1)S(1)}) custom-call(s32[2]{0:T(128)S(1)} %copy-done.31, bf16[768,1024]{1,0:T(8,128)(2,1)S(1)} %copy-done.8, bf16[512,768]{1,0:T(8,128)(2,1)S(1)} %copy-done.11, bf16[768,1024]{1,0:T(8,128)(2,1)S(1)} %copy-done.8, bf16[1024,768]{1,0:T(8,128)(2,1)S(1)} %copy-done.6, ...), custom_call_target="tpu_custom_call" | custom-call | flops 1000 | bytes 1000 | tf_op jit(solution)/shard_map/grad_columns/pallas_call | solution.py:879
  216.0 2.9 input_back.2.other_ref
  219.1 2.3 halve.5
  225.5 2.6 input_back.3.own_ref
  228.2 3.8 %small_sums.1 = f32[40,768]{1,0:T(8,128)S(1)} custom-call(f32[512,768]{1,0:T(8,128)S(1)} %input_back.3.own_ref, bf16[512,768]{1,0:T(8,128)(2,1)} %input_back.2.other_ref, bf16[512,768]{1,0:T(8,128)(2,1)S(1)} %bitcast.50, bf16[512,768]{1,0:T(8,128)(2,1)S(1)} %copy-done.2, f32[512,128]{1,0:T(8,128)S(1)} %copy-done.16, bf16[512,768]{1,0:T(8,128)(2,1)S(1)} %copy-done.11, ...), custom_call_target="tpu_custom_call" | custom-call | flops 1000 | bytes 1000 | tf_op jit(solution)/shard_map/small_sums/pallas_call | solution.py:970
  233.5 1.6 collective-permute-done.27.across_ref
  235.1 3.0 column_sends.2
  238.1 1.6 collective-permute-start.28
  239.7 6.9 %collective-permute-start.29 = (bf16[48,1920]{1,0:T(8,128)(2,1)S(1)}, bf16[48,1920]{1,0:T(8,128)(2,1)S(1)}, u32[]{:S(2)}, u32[]{:S(2)}) collective-permute-start(bf16[48,1920]{1,0:T(8,128)(2,1)S(1)} %get-tuple-element.195), channel_id=1, source_target_pairs={{0,4},{1,5},{2,6},{3,7},{4,0},{5,1},{6,2},{7,3},{8,12},{9,13},{10,... | collective-permute-start | bytes 552968 | tf_op jit(solution)/shard_map/ppermute | solution.py:404
  249.2 4.4 %collective-permute-done.25.across_ref = bf16[4,48,2304]{2,1,0:T(8,128)(2,1)} collective-permute-done((bf16[4,48,2304]{2,1,0:T(8,128)(2,1)}, bf16[4,48,2304]{2,1,0:T(8,128)(2,1)}, u32[]{:S(2)}, u32[]{:S(2)}) %collective-permute-start.25) | collective-permute-done | bytes 884768 | tf_op jit(solution)/shard_map/ppermute | solution.py:404
  255.1 3.1 %column_sends.3 = (f32[48,2304]{1,0:T(8,128)S(1)}, bf16[48,2304]{1,0:T(8,128)(2,1)S(1)}, bf16[48,2304]{1,0:T(8,128)(2,1)S(1)}, bf16[48,2304]{1,0:T(8,128)(2,1)S(1)}) custom-call(f32[4,48,2304]{2,1,0:T(8,128)S(1)} %copy-done.19, bf16[4,48,2304]{2,1,0:T(8,128)(2,1)} %collective-permute-done.25.across_ref), custom_call_target="tpu_custom_call" | custom-call | flops 1000 | bytes 1000 | tf_op jit(solution)/shard_map/column_sends/pallas_call | solution.py:1050
  258.2 2.8 state_back.1
  262.6 6.8 %collective-permute-start.34 = (bf16[48,2304]{1,0:T(8,128)(2,1)S(1)}, bf16[48,2304]{1,0:T(8,128)(2,1)S(1)}, u32[]{:S(2)}, u32[]{:S(2)}) collective-permute-start(bf16[48,2304]{1,0:T(8,128)(2,1)S(1)} %get-tuple-element.200), channel_id=1, source_target_pairs={{0,4},{1,5},{2,6},{3,7},{4,0},{5,1},{6,2},{7,3},{8,12},{9,13},{10,... | collective-permute-start | bytes 663560 | tf_op jit(solution)/shard_map/ppermute | solution.py:404
  270.3 1.6 collective-permute-start.36
  274.5 11.1 %collective-permute-done.33 = f32[40,768]{1,0:T(8,128)S(1)} collective-permute-done((f32[40,768]{1,0:T(8,128)S(1)}, f32[40,768]{1,0:T(8,128)S(1)}, u32[]{:S(2)}, u32[]{:S(2)}) %collective-permute-start.33) | collective-permute-done | bytes 122912 | tf_op jit(solution)/shard_map/ppermute | solution.py:404
  285.6 2.6 collective-permute-done.35
  288.3 4.3 %collective-permute-start.37 = (f32[40,768]{1,0:T(8,128)S(1)}, f32[40,768]{1,0:T(8,128)S(1)}, u32[]{:S(2)}, u32[]{:S(2)}) collective-permute-start(f32[40,768]{1,0:T(8,128)S(1)} %add.197), channel_id=1, source_target_pairs={{0,8},{1,9},{2,10},{3,11},{4,12},{5,13},{6,14},{7,15},{8,0},{9,1},... | collective-permute-start | bytes 368648 | tf_op jit(solution)/shard_map/ppermute | solution.py:404
  (283 shorter events, 61.5 us)
Async XLA Ops:
  7.2 110.4 %all-gather.2.cloned.1.call-start = ((), (), s32[]{:S(2)}) async-start(), calls=%async_computation.1 | async-start | bytes 5013504 | tf_op jit(solution)/shard_map/all_gather | solution.py:1208
  8.3 12.0 %collective-permute-start = (bf16[48,1152]{1,0:T(8,128)(2,1)S(1)}, bf16[48,1152]{1,0:T(8,128)(2,1)S(1)}, u32[]{:S(2)}, u32[]{:S(2)}) collective-permute-start(bf16[48,1152]{1,0:T(8,128)(2,1)S(1)} %get-tuple-element.229), channel_id=1, source_target_pairs={{0,4},{1,5},{2,6},{3,7},{4,0},{5,1},{6,2},{7,3},{8,12},{9,13},{10,... | collective-permute-start | bytes 331784 | tf_op jit(solution)/shard_map/ppermute | solution.py:404
  11.4 11.3 %collective-permute-start.1 = (bf16[48,1152]{1,0:T(8,128)(2,1)S(1)}, bf16[48,1152]{1,0:T(8,128)(2,1)S(1)}, u32[]{:S(2)}, u32[]{:S(2)}) collective-permute-start(bf16[48,1152]{1,0:T(8,128)(2,1)S(1)} %get-tuple-element.229), channel_id=1, source_target_pairs={{0,8},{1,9},{2,10},{3,11},{4,12},{5,13},{6,14},{7,15},{8,0},{9,1},... | collective-permute-start | bytes 331784 | tf_op jit(solution)/shard_map/ppermute | solution.py:404
  14.0 8.8 %collective-permute-start.2 = (bf16[48,1152]{1,0:T(8,128)(2,1)S(1)}, bf16[48,1152]{1,0:T(8,128)(2,1)S(1)}, u32[]{:S(2)}, u32[]{:S(2)}) collective-permute-start(bf16[48,1152]{1,0:T(8,128)(2,1)S(1)} %get-tuple-element.229), channel_id=1, source_target_pairs={{0,12},{1,13},{2,14},{3,15},{4,8},{5,9},{6,10},{7,11},{8,4},{9,5},... | collective-permute-start | bytes 331784 | tf_op jit(solution)/shard_map/ppermute | solution.py:404
  14.0 32.2 %collective-permute-start.3 = (bf16[512,768]{1,0:T(8,128)(2,1)}, bf16[512,768]{1,0:T(8,128)(2,1)S(1)}, u32[]{:S(2)}, u32[]{:S(2)}) collective-permute-start(bf16[512,768]{1,0:T(8,128)(2,1)} %bitcast.49), channel_id=1, source_target_pairs={{0,16},{16,0},{1,17},{17,1},{2,18},{18,2},{3,19},{19,3},{4,20},{20... | collective-permute-start | bytes 2359304 | tf_op jit(solution)/shard_map/ppermute | solution.py:1101
  20.3 40.5 %copy-start.30 = (s32[2]{0:T(128)}, s32[2]{0:T(128)S(1)}, u32[]{:S(2)}) copy-start(s32[2]{0:T(128)S(1)} %pad_add_fusion.1.place) | copy-start | bytes 28
  22.8 13.9 %collective-permute-start.4 = (bf16[4,48,1152]{2,1,0:T(8,128)(2,1)S(1)}, bf16[4,48,1152]{2,1,0:T(8,128)(2,1)}, u32[]{:S(2)}, u32[]{:S(2)}) collective-permute-start(bf16[4,48,1152]{2,1,0:T(8,128)(2,1)S(1)} %pad_maximum_fusion.2), channel_id=1, source_target_pairs={{0,2},{1,3},{2,0},{3,1},{4,6},{5,7},{6,4},{7,5},{8,10},{9,11},{10,... | collective-permute-start | bytes 1327112 | tf_op jit(solution)/shard_map/ppermute | solution.py:404
  24.4 14.9 %collective-permute-start.7 = (bf16[48,896]{1,0:T(8,128)(2,1)S(1)}, bf16[48,896]{1,0:T(8,128)(2,1)S(1)}, u32[]{:S(2)}, u32[]{:S(2)}) collective-permute-start(bf16[48,896]{1,0:T(8,128)(2,1)S(1)} %fusion.2), channel_id=1, source_target_pairs={{0,4},{1,5},{2,6},{3,7},{4,0},{5,1},{6,2},{7,3},{8,12},{9,13},{10,... | collective-permute-start | bytes 258056 | tf_op jit(solution)/shard_map/ppermute | solution.py:404
  26.2 13.2 %collective-permute-start.8 = (bf16[48,896]{1,0:T(8,128)(2,1)S(1)}, bf16[48,896]{1,0:T(8,128)(2,1)}, u32[]{:S(2)}, u32[]{:S(2)}) collective-permute-start(bf16[48,896]{1,0:T(8,128)(2,1)S(1)} %fusion.2), channel_id=1, source_target_pairs={{0,8},{1,9},{2,10},{3,11},{4,12},{5,13},{6,14},{7,15},{8,0},{9,1},... | collective-permute-start | bytes 258056 | tf_op jit(solution)/shard_map/ppermute | solution.py:404
  27.5 11.9 %collective-permute-start.9 = (bf16[48,896]{1,0:T(8,128)(2,1)S(1)}, bf16[48,896]{1,0:T(8,128)(2,1)}, u32[]{:S(2)}, u32[]{:S(2)}) collective-permute-start(bf16[48,896]{1,0:T(8,128)(2,1)S(1)} %fusion.2), channel_id=1, source_target_pairs={{0,12},{1,13},{2,14},{3,15},{4,8},{5,9},{6,10},{7,11},{8,4},{9,5},... | collective-permute-start | bytes 258056 | tf_op jit(solution)/shard_map/ppermute | solution.py:404
  30.0 203.5 %reduce-scatter.2.cloned.1.call-start = ((), (), s32[]{:S(2)}) async-start(), calls=%async_computation.2 | async-start | bytes 5013504 | tf_op jit(solution)/shard_map/reduce_scatter | solution.py:1243
  37.8 19.5 %collective-permute-start.6 = (bf16[8,48,1152]{2,1,0:T(8,128)(2,1)S(1)}, bf16[8,48,1152]{2,1,0:T(8,128)(2,1)S(1)}, u32[]{:S(2)}, u32[]{:S(2)}) collective-permute-start(bf16[8,48,1152]{2,1,0:T(8,128)(2,1)S(1)} %constant_dynamic-update-slice_fusion.refs_0_), channel_id=1, source_target_pairs={{0,16},{16,0},{1,17},{17,1},{2,18},{18,2},{3,19},{19,3},{4,20},{20... | collective-permute-start | bytes 2654216 | tf_op jit(solution)/shard_map/ppermute | solution.py:1101
  39.4 21.4 %collective-permute-start.5 = (bf16[8,48,1152]{2,1,0:T(8,128)(2,1)S(1)}, bf16[8,48,1152]{2,1,0:T(8,128)(2,1)S(1)}, u32[]{:S(2)}, u32[]{:S(2)}) collective-permute-start(bf16[8,48,1152]{2,1,0:T(8,128)(2,1)S(1)} %constant_dynamic-update-slice_fusion.refs_0_), channel_id=1, source_target_pairs={{0,1},{1,0},{2,3},{3,2},{4,5},{5,4},{6,7},{7,6},{8,9},{9,8},{10,11... | collective-permute-start | bytes 2654216 | tf_op jit(solution)/shard_map/ppermute | solution.py:404
  41.1 10.5 %collective-permute-start.10 = (bf16[4,48,896]{2,1,0:T(8,128)(2,1)S(1)}, bf16[4,48,896]{2,1,0:T(8,128)(2,1)S(1)}, u32[]{:S(2)}, u32[]{:S(2)}) collective-permute-start(bf16[4,48,896]{2,1,0:T(8,128)(2,1)S(1)} %pad_maximum_fusion.3), channel_id=1, source_target_pairs={{0,2},{1,3},{2,0},{3,1},{4,6},{5,7},{6,4},{7,5},{8,10},{9,11},{10,... | collective-permute-start | bytes 1032200 | tf_op jit(solution)/shard_map/ppermute | solution.py:404
  45.3 25.9 %collective-permute-start.12 = (bf16[48,2048]{1,0:T(8,128)(2,1)}, bf16[48,2048]{1,0:T(8,128)(2,1)S(1)}, u32[]{:S(2)}, u32[]{:S(2)}) collective-permute-start(bf16[48,2048]{1,0:T(8,128)(2,1)} %slice.152), channel_id=1, source_target_pairs={{0,4},{1,5},{2,6},{3,7},{4,0},{5,1},{6,2},{7,3},{8,12},{9,13},{10,... | collective-permute-start | bytes 589832 | tf_op jit(solution)/shard_map/ppermute | solution.py:404
  46.2 25.0 %collective-permute-start.13 = (bf16[48,2048]{1,0:T(8,128)(2,1)}, bf16[48,2048]{1,0:T(8,128)(2,1)S(1)}, u32[]{:S(2)}, u32[]{:S(2)}) collective-permute-start(bf16[48,2048]{1,0:T(8,128)(2,1)} %slice.152), channel_id=1, source_target_pairs={{0,8},{1,9},{2,10},{3,11},{4,12},{5,13},{6,14},{7,15},{8,0},{9,1},... | collective-permute-start | bytes 589832 | tf_op jit(solution)/shard_map/ppermute | solution.py:404
  51.6 19.6 %collective-permute-start.14 = (bf16[48,2048]{1,0:T(8,128)(2,1)}, bf16[48,2048]{1,0:T(8,128)(2,1)S(1)}, u32[]{:S(2)}, u32[]{:S(2)}) collective-permute-start(bf16[48,2048]{1,0:T(8,128)(2,1)} %slice.152), channel_id=1, source_target_pairs={{0,12},{1,13},{2,14},{3,15},{4,8},{5,9},{6,10},{7,11},{8,4},{9,5},... | collective-permute-start | bytes 589832 | tf_op jit(solution)/shard_map/ppermute | solution.py:404
  57.3 3.5 %collective-permute-start.11 = (bf16[8,48,1152]{2,1,0:T(8,128)(2,1)S(1)}, bf16[8,48,1152]{2,1,0:T(8,128)(2,1)S(1)}, u32[]{:S(2)}, u32[]{:S(2)}) collective-permute-start(bf16[8,48,1152]{2,1,0:T(8,128)(2,1)S(1)} %collective-permute-done.6.refs_2_), channel_id=1, source_target_pairs={{0,1},{1,0},{2,3},{3,2},{4,5},{5,4},{6,7},{7,6},{8,9},{9,8},{10,11... | collective-permute-start | bytes 2654216 | tf_op jit(solution)/shard_map/ppermute | solution.py:404
  73.1 20.2 %collective-permute-start.19 = (bf16[4,48,2048]{2,1,0:T(8,128)(2,1)}, bf16[4,48,2048]{2,1,0:T(8,128)(2,1)}, u32[]{:S(2)}, u32[]{:S(2)}) collective-permute-start(bf16[4,48,2048]{2,1,0:T(8,128)(2,1)} %pad_maximum_fusion.1.refs_4_), channel_id=1, source_target_pairs={{0,2},{1,3},{2,0},{3,1},{4,6},{5,7},{6,4},{7,5},{8,10},{9,11},{10,... | collective-permute-start | bytes 2359304 | tf_op jit(solution)/shard_map/ppermute | solution.py:404
  73.5 20.3 %collective-permute-start.16 = (bf16[8,48,896]{2,1,0:T(8,128)(2,1)}, bf16[8,48,896]{2,1,0:T(8,128)(2,1)}, u32[]{:S(2)}, u32[]{:S(2)}) collective-permute-start(bf16[8,48,896]{2,1,0:T(8,128)(2,1)} %constant_dynamic-update-slice_fusion.5.refs_0_), channel_id=1, source_target_pairs={{0,16},{16,0},{1,17},{17,1},{2,18},{18,2},{3,19},{19,3},{4,20},{20... | collective-permute-start | bytes 2064392 | tf_op jit(solution)/shard_map/ppermute | solution.py:1101
  75.0 22.9 %collective-permute-start.18 = (bf16[4,48,2048]{2,1,0:T(8,128)(2,1)}, bf16[4,48,2048]{2,1,0:T(8,128)(2,1)}, u32[]{:S(2)}, u32[]{:S(2)}) collective-permute-start(bf16[4,48,2048]{2,1,0:T(8,128)(2,1)} %pad_maximum_fusion.1.refs_4_), channel_id=1, source_target_pairs={{0,1},{1,0},{2,3},{3,2},{4,5},{5,4},{6,7},{7,6},{8,9},{9,8},{10,11... | collective-permute-start | bytes 2359304 | tf_op jit(solution)/shard_map/ppermute | solution.py:404
  93.3 4.6 %collective-permute-start.20 = (bf16[4,48,2048]{2,1,0:T(8,128)(2,1)}, bf16[4,48,2048]{2,1,0:T(8,128)(2,1)}, u32[]{:S(2)}, u32[]{:S(2)}) collective-permute-start(bf16[4,48,2048]{2,1,0:T(8,128)(2,1)} %collective-permute-done.19.refs_6_), channel_id=1, source_target_pairs={{0,1},{1,0},{2,3},{3,2},{4,5},{5,4},{6,7},{7,6},{8,9},{9,8},{10,11... | collective-permute-start | bytes 2359304 | tf_op jit(solution)/shard_map/ppermute | solution.py:404
  93.3 3.6 %collective-permute-start.15 = (bf16[8,48,896]{2,1,0:T(8,128)(2,1)}, bf16[8,48,896]{2,1,0:T(8,128)(2,1)}, u32[]{:S(2)}, u32[]{:S(2)}) collective-permute-start(bf16[8,48,896]{2,1,0:T(8,128)(2,1)} %constant_dynamic-update-slice_fusion.5.refs_0_), channel_id=1, source_target_pairs={{0,1},{1,0},{2,3},{3,2},{4,5},{5,4},{6,7},{7,6},{8,9},{9,8},{10,11... | collective-permute-start | bytes 2064392 | tf_op jit(solution)/shard_map/ppermute | solution.py:404
  93.9 4.1 %collective-permute-start.17 = (bf16[8,48,896]{2,1,0:T(8,128)(2,1)}, bf16[8,48,896]{2,1,0:T(8,128)(2,1)}, u32[]{:S(2)}, u32[]{:S(2)}) collective-permute-start(bf16[8,48,896]{2,1,0:T(8,128)(2,1)} %collective-permute-done.16.refs_2_), channel_id=1, source_target_pairs={{0,1},{1,0},{2,3},{3,2},{4,5},{5,4},{6,7},{7,6},{8,9},{9,8},{10,11... | collective-permute-start | bytes 2064392 | tf_op jit(solution)/shard_map/ppermute | solution.py:404
  159.5 5.4 %collective-permute-start.21 = (bf16[8,48,3840]{2,1,0:T(8,128)(2,1)S(1)}, bf16[8,48,3840]{2,1,0:T(8,128)(2,1)S(1)}, u32[]{:S(2)}, u32[]{:S(2)}) collective-permute-start(bf16[8,48,3840]{2,1,0:T(8,128)(2,1)S(1)} %get-tuple-element.169), channel_id=1, source_target_pairs={{0,1},{1,0},{2,3},{3,2},{4,5},{5,4},{6,7},{7,6},{8,9},{9,8},{10,11... | collective-permute-start | bytes 8847368 | tf_op jit(solution)/shard_map/ppermute | solution.py:404
  169.6 34.6 %collective-permute-start.22 = (bf16[8,48,1920]{2,1,0:T(8,128)(2,1)}, bf16[8,48,1920]{2,1,0:T(8,128)(2,1)}, u32[]{:S(2)}, u32[]{:S(2)}) collective-permute-start(bf16[8,48,1920]{2,1,0:T(8,128)(2,1)} %get-tuple-element.170), channel_id=1, source_target_pairs={{0,16},{16,0},{1,17},{17,1},{2,18},{18,2},{3,19},{19,3},{4,20},{20... | collective-permute-start | bytes 4423688 | tf_op jit(solution)/shard_map/ppermute | solution.py:1101
  215.3 3.8 %collective-permute-start.23 = (bf16[8,48,2304]{2,1,0:T(8,128)(2,1)S(1)}, bf16[8,48,2304]{2,1,0:T(8,128)(2,1)S(1)}, u32[]{:S(2)}, u32[]{:S(2)}) collective-permute-start(bf16[8,48,2304]{2,1,0:T(8,128)(2,1)S(1)} %get-tuple-element.181), channel_id=1, source_target_pairs={{0,1},{1,0},{2,3},{3,2},{4,5},{5,4},{6,7},{7,6},{8,9},{9,8},{10,11... | collective-permute-start | bytes 5308424 | tf_op jit(solution)/shard_map/ppermute | solution.py:404
  215.4 19.7 %collective-permute-start.27 = (bf16[4,48,1920]{2,1,0:T(8,128)(2,1)}, bf16[4,48,1920]{2,1,0:T(8,128)(2,1)}, u32[]{:S(2)}, u32[]{:S(2)}) collective-permute-start(bf16[4,48,1920]{2,1,0:T(8,128)(2,1)} %get-tuple-element.178), channel_id=1, source_target_pairs={{0,2},{1,3},{2,0},{3,1},{4,6},{5,7},{6,4},{7,5},{8,10},{9,11},{10,... | collective-permute-start | bytes 2211848 | tf_op jit(solution)/shard_map/ppermute | solution.py:404
  222.6 31.0 %collective-permute-start.25 = (bf16[4,48,2304]{2,1,0:T(8,128)(2,1)}, bf16[4,48,2304]{2,1,0:T(8,128)(2,1)}, u32[]{:S(2)}, u32[]{:S(2)}) collective-permute-start(bf16[4,48,2304]{2,1,0:T(8,128)(2,1)} %get-tuple-element.185), channel_id=1, source_target_pairs={{0,2},{1,3},{2,0},{3,1},{4,6},{5,7},{6,4},{7,5},{8,10},{9,11},{10,... | collective-permute-start | bytes 2654216 | tf_op jit(solution)/shard_map/ppermute | solution.py:404
  223.9 34.3 %collective-permute-start.24 = (bf16[512,768]{1,0:T(8,128)(2,1)}, bf16[512,768]{1,0:T(8,128)(2,1)}, u32[]{:S(2)}, u32[]{:S(2)}) collective-permute-start(bf16[512,768]{1,0:T(8,128)(2,1)} %input_back.2.other_ref), channel_id=1, source_target_pairs={{0,16},{16,0},{1,17},{17,1},{2,18},{18,2},{3,19},{19,3},{4,20},{20... | collective-permute-start | bytes 2359304 | tf_op jit(solution)/shard_map/ppermute | solution.py:1101
  232.0 23.1 %copy-start.19 = (f32[4,48,2304]{2,1,0:T(8,128)S(1)}, f32[4,48,2304]{2,1,0:T(8,128)}, u32[]{:S(2)}) copy-start(f32[4,48,2304]{2,1,0:T(8,128)} %copy-done.18) | copy-start | bytes 5308420
  232.0 1.4 collective-permute-start.26
  238.1 20.2 %copy-start.5 = (f32[512,768]{1,0:T(8,128)S(1)}, f32[512,768]{1,0:T(8,128)}, u32[]{:S(2)}) copy-start(f32[512,768]{1,0:T(8,128)} %copy-done.4) | copy-start | bytes 4718596
  238.1 20.2 %copy-start.17 = (f32[512,128]{1,0:T(8,128)S(1)}, f32[512,128]{1,0:T(8,128)}, u32[]{:S(2)}) copy-start(f32[512,128]{1,0:T(8,128)} %pad_convert_fusion.mask_ref) | copy-start | bytes 786436
  238.1 20.2 %copy-start.28 = (f32[8,768]{1,0:T(8,128)S(1)}, f32[8,768]{1,0:T(8,128)}, u32[]{:S(2)}) copy-start(f32[8,768]{1,0:T(8,128)} %pad.39.tap_ref) | copy-start | bytes 73732
  238.1 9.6 %collective-permute-start.28 = (f32[40,768]{1,0:T(8,128)S(1)}, f32[40,768]{1,0:T(8,128)S(1)}, u32[]{:S(2)}, u32[]{:S(2)}) collective-permute-start(f32[40,768]{1,0:T(8,128)S(1)} %add.191), channel_id=1, source_target_pairs={{0,16},{16,0},{1,17},{17,1},{2,18},{18,2},{3,19},{19,3},{4,20},{20... | collective-permute-start | bytes 368648 | tf_op jit(solution)/shard_map/ppermute | solution.py:1101
  239.7 21.4 %collective-permute-start.29 = (bf16[48,1920]{1,0:T(8,128)(2,1)S(1)}, bf16[48,1920]{1,0:T(8,128)(2,1)S(1)}, u32[]{:S(2)}, u32[]{:S(2)}) collective-permute-start(bf16[48,1920]{1,0:T(8,128)(2,1)S(1)} %get-tuple-element.195), channel_id=1, source_target_pairs={{0,4},{1,5},{2,6},{3,7},{4,0},{5,1},{6,2},{7,3},{8,12},{9,13},{10,... | collective-permute-start | bytes 552968 | tf_op jit(solution)/shard_map/ppermute | solution.py:404
  246.6 14.5 %collective-permute-start.30 = (bf16[48,1920]{1,0:T(8,128)(2,1)S(1)}, bf16[48,1920]{1,0:T(8,128)(2,1)S(1)}, u32[]{:S(2)}, u32[]{:S(2)}) collective-permute-start(bf16[48,1920]{1,0:T(8,128)(2,1)S(1)} %get-tuple-element.196), channel_id=1, source_target_pairs={{0,8},{1,9},{2,10},{3,11},{4,12},{5,13},{6,14},{7,15},{8,0},{9,1},... | collective-permute-start | bytes 552968 | tf_op jit(solution)/shard_map/ppermute | solution.py:404
  247.7 13.4 %collective-permute-start.31 = (bf16[48,1920]{1,0:T(8,128)(2,1)S(1)}, bf16[48,1920]{1,0:T(8,128)(2,1)S(1)}, u32[]{:S(2)}, u32[]{:S(2)}) collective-permute-start(bf16[48,1920]{1,0:T(8,128)(2,1)S(1)} %get-tuple-element.197), channel_id=1, source_target_pairs={{0,12},{1,13},{2,14},{3,15},{4,8},{5,9},{6,10},{7,11},{8,4},{9,5},... | collective-permute-start | bytes 552968 | tf_op jit(solution)/shard_map/ppermute | solution.py:404
  253.6 18.7 %collective-permute-start.40 = (bf16[192,768]{1,0:T(8,128)(2,1)S(1)}, bf16[192,768]{1,0:T(8,128)(2,1)S(1)}, u32[]{:S(2)}, u32[]{:S(2)}) collective-permute-start(bf16[192,768]{1,0:T(8,128)(2,1)S(1)} %copy-done.40), channel_id=1, source_target_pairs={{0,16},{16,0},{1,17},{17,1},{2,18},{18,2},{3,19},{19,3},{4,20},{20... | collective-permute-start | bytes 884744 | tf_op jit(solution)/shard_map/ppermute | solution.py:1101
  261.2 10.7 %collective-permute-start.32 = (f32[40,768]{1,0:T(8,128)S(1)}, f32[40,768]{1,0:T(8,128)S(1)}, u32[]{:S(2)}, u32[]{:S(2)}) collective-permute-start(f32[40,768]{1,0:T(8,128)S(1)} %add.192), channel_id=1, source_target_pairs={{0,2},{1,3},{2,0},{3,1},{4,6},{5,7},{6,4},{7,5},{8,10},{9,11},{10,... | collective-permute-start | bytes 368648 | tf_op jit(solution)/shard_map/ppermute | solution.py:404
  262.6 23.0 %collective-permute-start.34 = (bf16[48,2304]{1,0:T(8,128)(2,1)S(1)}, bf16[48,2304]{1,0:T(8,128)(2,1)S(1)}, u32[]{:S(2)}, u32[]{:S(2)}) collective-permute-start(bf16[48,2304]{1,0:T(8,128)(2,1)S(1)} %get-tuple-element.200), channel_id=1, source_target_pairs={{0,4},{1,5},{2,6},{3,7},{4,0},{5,1},{6,2},{7,3},{8,12},{9,13},{10,... | collective-permute-start | bytes 663560 | tf_op jit(solution)/shard_map/ppermute | solution.py:404
  269.5 18.7 %collective-permute-start.35 = (bf16[48,2304]{1,0:T(8,128)(2,1)S(1)}, bf16[48,2304]{1,0:T(8,128)(2,1)S(1)}, u32[]{:S(2)}, u32[]{:S(2)}) collective-permute-start(bf16[48,2304]{1,0:T(8,128)(2,1)S(1)} %get-tuple-element.201), channel_id=1, source_target_pairs={{0,8},{1,9},{2,10},{3,11},{4,12},{5,13},{6,14},{7,15},{8,0},{9,1},... | collective-permute-start | bytes 663560 | tf_op jit(solution)/shard_map/ppermute | solution.py:404
  270.3 18.0 %collective-permute-start.36 = (bf16[48,2304]{1,0:T(8,128)(2,1)S(1)}, bf16[48,2304]{1,0:T(8,128)(2,1)S(1)}, u32[]{:S(2)}, u32[]{:S(2)}) collective-permute-start(bf16[48,2304]{1,0:T(8,128)(2,1)S(1)} %get-tuple-element.202), channel_id=1, source_target_pairs={{0,12},{1,13},{2,14},{3,15},{4,8},{5,9},{6,10},{7,11},{8,4},{9,5},... | collective-permute-start | bytes 663560 | tf_op jit(solution)/shard_map/ppermute | solution.py:404
  271.8 20.8 %collective-permute-start.39 = (bf16[48,1920]{1,0:T(8,128)(2,1)S(1)}, bf16[48,1920]{1,0:T(8,128)(2,1)S(1)}, u32[]{:S(2)}, u32[]{:S(2)}) collective-permute-start(bf16[48,1920]{1,0:T(8,128)(2,1)S(1)} %add_convert_fusion.4), channel_id=1, source_target_pairs={{0,16},{16,0},{1,17},{17,1},{2,18},{18,2},{3,19},{19,3},{4,20},{20... | collective-permute-start | bytes 552968 | tf_op jit(solution)/shard_map/ppermute | solution.py:1101
  272.3 13.3 %collective-permute-start.33 = (f32[40,768]{1,0:T(8,128)S(1)}, f32[40,768]{1,0:T(8,128)S(1)}, u32[]{:S(2)}, u32[]{:S(2)}) collective-permute-start(f32[40,768]{1,0:T(8,128)S(1)} %add.196), channel_id=1, source_target_pairs={{0,4},{1,5},{2,6},{3,7},{4,0},{5,1},{6,2},{7,3},{8,12},{9,13},{10,... | collective-permute-start | bytes 368648 | tf_op jit(solution)/shard_map/ppermute | solution.py:404
  288.3 7.1 %collective-permute-start.37 = (f32[40,768]{1,0:T(8,128)S(1)}, f32[40,768]{1,0:T(8,128)S(1)}, u32[]{:S(2)}, u32[]{:S(2)}) collective-permute-start(f32[40,768]{1,0:T(8,128)S(1)} %add.197), channel_id=1, source_target_pairs={{0,8},{1,9},{2,10},{3,11},{4,12},{5,13},{6,14},{7,15},{8,0},{9,1},... | collective-permute-start | bytes 368648 | tf_op jit(solution)/shard_map/ppermute | solution.py:404
  294.2 5.9 %collective-permute-start.38 = (bf16[48,2304]{1,0:T(8,128)(2,1)S(1)}, bf16[48,2304]{1,0:T(8,128)(2,1)S(1)}, u32[]{:S(2)}, u32[]{:S(2)}) collective-permute-start(bf16[48,2304]{1,0:T(8,128)(2,1)S(1)} %add_convert_fusion.3), channel_id=1, source_target_pairs={{0,16},{16,0},{1,17},{17,1},{2,18},{18,2},{3,19},{19,3},{4,20},{20... | collective-permute-start | bytes 663560 | tf_op jit(solution)/shard_map/ppermute | solution.py:1101
  (57 other events, 413.5 us)
Sparse Core Ops, SparseCore 0:
  30.1 59.1 all-gather.1
  134.2 83.2 reduce-scatter.1
